TPU v7x, 32 devices: a whole 2x2x4 slice. The times are simulated.
32 devices in a mesh: rep: 8 (over y, x, core), shard: 4 (over z).
Axes of the slice: x: 2, y: 2, z: 4, core: 2. Of those that a mesh axis runs over, the one named last changes fastest.
Arguments:
- tokens: bfloat16 [16, 1024, 768], P('rep', 'shard'), may hold values from -6 to 6
- gain_attn: bfloat16 [768], P('shard'), may hold values from 0.25 to 1.75
- bias_attn: bfloat16 [768], P('shard'), may hold values from -1.5 to 1.5
- w_qkv: bfloat16 [768, 2304], P('shard'), may hold values from -0.21875 to 0.21875
- w_feature: bfloat16 [768, 128], P('shard'), may hold values from -1.5 to 1.5
- w_out: bfloat16 [768, 768], P('shard'), may hold values from -0.875 to 0.875
- gain_mlp: bfloat16 [768], P('shard'), may hold values from 0.25 to 1.75
- bias_mlp: bfloat16 [768], P('shard'), may hold values from -1.5 to 1.5
- w_up: bfloat16 [768, 3072], P('shard'), may hold values from -0.21875 to 0.21875
- w_down: bfloat16 [3072, 768], P('shard'), may hold values from -0.109375 to 0.109375
- cotangent: bfloat16 [16, 1024, 768], P('rep', 'shard'), may hold values from -6 to 6
Outputs:
- block_out: bfloat16 [16, 1024, 768], P('rep', 'shard')
- grad_tokens: bfloat16 [16, 1024, 768], P('rep', 'shard')
- grad_gain_attn: float32 [768], P('shard')
- grad_bias_attn: float32 [768], P('shard')
- grad_w_qkv: float32 [768, 2304], P('shard')
- grad_w_feature: float32 [768, 128], P('shard')
- grad_w_out: float32 [768, 768], P('shard')
- grad_gain_mlp: float32 [768], P('shard')
- grad_bias_mlp: float32 [768], P('shard')
- grad_w_up: float32 [768, 3072], P('shard')
- grad_w_down: float32 [3072, 768], P('shard')
All inputs are finite; a program needn't handle non-finite values.
Results may differ from a plain program's by a relative error of at most 0.019.
Values may be sent and summed in bfloat16 or wider, within the bound.
No kernel may reach another device: no remote copies, remote signals or barrier semaphores. Data moves between devices by JAX's collectives and lax.ppermute only.
A program may use at most 192 MiB of HBM per device.

v0:
```python
import jax
import jax.numpy as jnp
from jax import lax
from jax.sharding import PartitionSpec as P

D = 768
HEADS = 12
HEAD = 64
FEAT = 128
STRETCH = 64


top_precision = lax.Precision.HIGHEST
norm_epsilon = 1e-05


def prefix(value, axis, combine, identity):
    count, here = (lax.axis_size(axis), lax.axis_index(axis))
    everything = jax.tree.map(
        lambda part, kind: lax.all_gather(part.astype(kind), axis),
        value,
        (jnp.bfloat16, jnp.bfloat16),
    )
    start = jax.tree.map(
        lambda part, zero: jnp.broadcast_to(jnp.asarray(zero, part.dtype), part.shape),
        value,
        identity,
    )

    def lap(k, before):
        reached = k < here
        new = combine(
            before, jax.tree.map(lambda part, own: part[k].astype(own.dtype), everything, value)
        )
        return jax.tree.map(lambda a, b: jnp.where(reached, a, b), new, before)

    return lax.fori_loop(0, count, lap, start)


def prefix_2(value, axis, join, neutral):
    count = lax.axis_size(axis)
    place = lax.axis_index(axis)
    ahead = count - 1 - place
    gathered = jax.tree.map(
        lambda a, kind: lax.all_gather(a.astype(kind), axis),
        value,
        jax.tree.map(lambda a: jnp.bfloat16 if a.dtype == jnp.float32 else a.dtype, value),
    )
    state = jax.tree.map(lambda a, e: jnp.zeros_like(a) + jnp.asarray(e, a.dtype), value, neutral)

    def one(lap, state):
        source = count - 1 - lap
        return join(
            state,
            jax.tree.map(
                lambda a, own: lax.dynamic_index_in_dim(a, source, 0, False).astype(own.dtype),
                gathered,
                value,
            ),
        )

    return lax.fori_loop(0, ahead, one, state)


def layer_norm(rows_in, gain, offset):
    centred = rows_in - jnp.mean(rows_in, axis=-1, keepdims=True)
    spread = jnp.mean(centred * centred, axis=-1, keepdims=True)
    return centred * lax.rsqrt(spread + norm_epsilon) * gain + offset


def featurize(inputs):
    return jnp.concatenate(
        [jax.nn.softmax(inputs, axis=-1), jax.nn.softmax(-inputs, axis=-1)], axis=-1
    )


def featurize_pair(u_query, u_key):
    return (featurize(u_query), featurize(u_key))


def gelu_tanh(pre_act):
    return jax.nn.gelu(pre_act, approximate=True)


def add_states(earlier, later):
    return jax.tree.map(jnp.add, earlier, later)


def shifted_sum(terms):
    running = jnp.cumsum(terms, axis=0)
    return jnp.concatenate([jnp.zeros_like(terms[:1]), running[:-1]], axis=0)


def attend_local(query_wide, key_wide, value_wide, prior_state, prior_total):
    length = query_wide.shape[0]
    blocks = length // STRETCH
    block_q = query_wide.reshape(blocks, STRETCH, HEADS, FEAT)
    block_k = key_wide.reshape(blocks, STRETCH, HEADS, FEAT)
    block_v = value_wide.reshape(blocks, STRETCH, HEADS, HEAD)
    state_terms = jnp.einsum("nshf,nshe->nhfe", block_k, block_v, precision=top_precision)
    total_terms = jnp.sum(block_k, axis=1)
    state_before = prior_state[None] + shifted_sum(state_terms)
    total_before = prior_total[None] + shifted_sum(total_terms)
    positions = jnp.arange(STRETCH)
    causal = positions[:, None] >= positions[None, :]
    scores = jnp.where(
        causal, jnp.einsum("nthf,nshf->nhts", block_q, block_k, precision=top_precision), 0.0
    )
    numerator = jnp.einsum("nhts,nshe->nthe", scores, block_v, precision=top_precision)
    numerator = numerator + jnp.einsum(
        "nthf,nhfe->nthe", block_q, state_before, precision=top_precision
    )
    denominator = jnp.transpose(jnp.sum(scores, axis=3), (0, 2, 1))
    denominator = denominator + jnp.einsum(
        "nthf,nhf->nth", block_q, total_before, precision=top_precision
    )
    return (numerator / denominator[..., None]).reshape(length, HEADS, HEAD)


def shards(
    tokens,
    gain_attn,
    bias_attn,
    w_qkv,
    w_feature,
    w_out,
    gain_mlp,
    bias_mlp,
    w_up,
    w_down,
    cotangent,
):
    shard_count = lax.axis_size("shard")
    local_weights = (
        gain_attn,
        bias_attn,
        w_qkv,
        w_feature,
        w_out,
        gain_mlp,
        bias_mlp,
        w_up,
        w_down,
    )
    totals = [
        jnp.zeros((weight.shape[0] * shard_count,) + weight.shape[1:], jnp.float32)
        for weight in local_weights
    ]
    results = []
    input_grads = []
    for batch_index in range(tokens.shape[0]):
        forward_set = (
            lax.all_gather(gain_attn, "shard", axis=0, tiled=True),
            lax.all_gather(bias_attn, "shard", axis=0, tiled=True),
            lax.all_gather(w_qkv, "shard", axis=0, tiled=True),
            lax.all_gather(w_feature, "shard", axis=0, tiled=True),
            lax.all_gather(w_out, "shard", axis=0, tiled=True),
            lax.all_gather(gain_mlp, "shard", axis=0, tiled=True),
            lax.all_gather(bias_mlp, "shard", axis=0, tiled=True),
            lax.all_gather(w_up, "shard", axis=0, tiled=True),
            lax.all_gather(w_down, "shard", axis=0, tiled=True),
        )
        (
            gain_one,
            bias_one,
            qkv_weight,
            feature_weight,
            out_weight,
            gain_two,
            bias_two,
            up_weight,
            down_weight,
        ) = forward_set
        rows_in = tokens[batch_index].astype(jnp.float32)
        length = rows_in.shape[0]
        normed, norm_pull = jax.vjp(
            layer_norm, rows_in, gain_one.astype(jnp.float32), bias_one.astype(jnp.float32)
        )
        normed_low = normed.astype(jnp.bfloat16)
        mixed = jnp.dot(normed_low, qkv_weight, preferred_element_type=jnp.float32).astype(
            jnp.bfloat16
        )
        queries = mixed[:, :D].reshape(length, HEADS, HEAD)
        key_rows = mixed[:, D : 2 * D].reshape(length, HEADS, HEAD)
        values = mixed[:, 2 * D :].reshape(length, HEADS, HEAD)
        feature_maps = feature_weight.reshape(HEADS, HEAD, 2, HEAD)
        u_query = jnp.einsum(
            "thi,hio->tho", queries, feature_maps[:, :, 0], preferred_element_type=jnp.float32
        )
        u_key = jnp.einsum(
            "thi,hio->tho", key_rows, feature_maps[:, :, 1], preferred_element_type=jnp.float32
        )
        (f_query, f_key), feature_pull = jax.vjp(featurize_pair, u_query, u_key)
        query_low = f_query.astype(jnp.bfloat16)
        key_low = f_key.astype(jnp.bfloat16)
        query_wide = query_low.astype(jnp.float32)
        key_wide = key_low.astype(jnp.float32)
        value_wide = values.astype(jnp.float32)
        key_state = jnp.einsum("shf,she->hfe", key_low, values, preferred_element_type=jnp.float32)
        key_sum = jnp.sum(key_wide, axis=0)
        prior = prefix(
            (key_state, key_sum),
            "shard",
            add_states,
            (jnp.zeros_like(key_state), jnp.zeros_like(key_sum)),
        )
        attended, attend_pull = jax.vjp(
            attend_local, query_wide, key_wide, value_wide, prior[0], prior[1]
        )
        attended_low = attended.reshape(length, D).astype(jnp.bfloat16)
        resid = rows_in + jnp.dot(attended_low, out_weight, preferred_element_type=jnp.float32)
        normed_two, norm_two_pull = jax.vjp(
            layer_norm, resid, gain_two.astype(jnp.float32), bias_two.astype(jnp.float32)
        )
        normed_two_low = normed_two.astype(jnp.bfloat16)
        pre_act = jnp.dot(normed_two_low, up_weight, preferred_element_type=jnp.float32)
        hidden, gelu_pull = jax.vjp(gelu_tanh, pre_act)
        hidden_low = hidden.astype(jnp.bfloat16)
        result = resid + jnp.dot(hidden_low, down_weight, preferred_element_type=jnp.float32)
        results.append(result.astype(jnp.bfloat16))
        qkv_back, feature_back, out_back, up_back, down_back = (
            lax.all_gather(w_qkv, "shard", axis=0, tiled=True),
            lax.all_gather(w_feature, "shard", axis=0, tiled=True),
            lax.all_gather(w_out, "shard", axis=0, tiled=True),
            lax.all_gather(w_up, "shard", axis=0, tiled=True),
            lax.all_gather(w_down, "shard", axis=0, tiled=True),
        )
        grad_out = cotangent[batch_index]
        d_down = jnp.dot(hidden_low.T, grad_out, preferred_element_type=jnp.float32)
        d_hidden = jnp.dot(grad_out, down_back.T, preferred_element_type=jnp.float32)
        (d_pre,) = gelu_pull(d_hidden)
        d_pre_low = d_pre.astype(jnp.bfloat16)
        d_up = jnp.dot(normed_two_low.T, d_pre_low, preferred_element_type=jnp.float32)
        d_normed_two = jnp.dot(d_pre_low, up_back.T, preferred_element_type=jnp.float32)
        d_resid_two, d_gain_two, d_bias_two = norm_two_pull(d_normed_two)
        d_resid = grad_out.astype(jnp.float32) + d_resid_two
        d_resid_low = d_resid.astype(jnp.bfloat16)
        d_out = jnp.dot(attended_low.T, d_resid_low, preferred_element_type=jnp.float32)
        d_attended = jnp.dot(d_resid_low, out_back.T, preferred_element_type=jnp.float32).reshape(
            length, HEADS, HEAD
        )
        d_query_f, d_key_f, d_value_f, local_state, local_sum = attend_pull(d_attended)
        later = prefix_2(
            (local_state, local_sum),
            "shard",
            add_states,
            (jnp.zeros_like(local_state), jnp.zeros_like(local_sum)),
        )
        d_key_f = (
            d_key_f
            + jnp.einsum("hfe,she->shf", later[0], value_wide, precision=top_precision)
            + later[1][None]
        )
        d_value_f = d_value_f + jnp.einsum(
            "hfe,shf->she", later[0], key_wide, precision=top_precision
        )
        d_u_query, d_u_key = feature_pull((d_query_f, d_key_f))
        d_uq_low = d_u_query.astype(jnp.bfloat16)
        d_uk_low = d_u_key.astype(jnp.bfloat16)
        back_maps = feature_back.reshape(HEADS, HEAD, 2, HEAD)
        d_queries = jnp.einsum(
            "tho,hio->thi", d_uq_low, back_maps[:, :, 0], preferred_element_type=jnp.float32
        )
        d_keys = jnp.einsum(
            "tho,hio->thi", d_uk_low, back_maps[:, :, 1], preferred_element_type=jnp.float32
        )
        query_map_grad = jnp.einsum(
            "thi,tho->hio", queries, d_uq_low, preferred_element_type=jnp.float32
        )
        key_map_grad = jnp.einsum(
            "thi,tho->hio", key_rows, d_uk_low, preferred_element_type=jnp.float32
        )
        d_maps = jnp.stack([query_map_grad, key_map_grad], axis=2).reshape(D, FEAT)
        d_mixed = jnp.concatenate(
            [d_queries.reshape(length, D), d_keys.reshape(length, D), d_value_f.reshape(length, D)],
            axis=1,
        ).astype(jnp.bfloat16)
        d_qkv = jnp.dot(normed_low.T, d_mixed, preferred_element_type=jnp.float32)
        d_normed = jnp.dot(d_mixed, qkv_back.T, preferred_element_type=jnp.float32)
        d_rows, d_gain_one, d_bias_one = norm_pull(d_normed)
        input_grads.append((d_resid + d_rows).astype(jnp.bfloat16))
        contributions = (
            d_gain_one,
            d_bias_one,
            d_qkv,
            d_maps,
            d_out,
            d_gain_two,
            d_bias_two,
            d_up,
            d_down,
        )
        totals = [total_sum + new_term for total_sum, new_term in zip(totals, contributions)]
    shares = (
        lax.psum_scatter(
            totals[0].astype(jnp.bfloat16), "shard", scatter_dimension=0, tiled=True
        ).astype(jnp.float32),
        lax.psum_scatter(
            totals[1].astype(jnp.bfloat16), "shard", scatter_dimension=0, tiled=True
        ).astype(jnp.float32),
        lax.psum_scatter(
            totals[2].astype(jnp.bfloat16), "shard", scatter_dimension=0, tiled=True
        ).astype(jnp.float32),
        lax.psum_scatter(
            totals[3].astype(jnp.bfloat16), "shard", scatter_dimension=0, tiled=True
        ).astype(jnp.float32),
        lax.psum_scatter(
            totals[4].astype(jnp.bfloat16), "shard", scatter_dimension=0, tiled=True
        ).astype(jnp.float32),
        lax.psum_scatter(
            totals[5].astype(jnp.bfloat16), "shard", scatter_dimension=0, tiled=True
        ).astype(jnp.float32),
        lax.psum_scatter(
            totals[6].astype(jnp.bfloat16), "shard", scatter_dimension=0, tiled=True
        ).astype(jnp.float32),
        lax.psum_scatter(
            totals[7].astype(jnp.bfloat16), "shard", scatter_dimension=0, tiled=True
        ).astype(jnp.float32),
        lax.psum_scatter(
            totals[8].astype(jnp.bfloat16), "shard", scatter_dimension=0, tiled=True
        ).astype(jnp.float32),
    )
    reduced = (
        lax.psum(shares[0].astype(jnp.bfloat16), "rep").astype(jnp.float32),
        lax.psum(shares[1].astype(jnp.bfloat16), "rep").astype(jnp.float32),
        lax.psum(shares[2].astype(jnp.bfloat16), "rep").astype(jnp.float32),
        lax.psum(shares[3].astype(jnp.bfloat16), "rep").astype(jnp.float32),
        lax.psum(shares[4].astype(jnp.bfloat16), "rep").astype(jnp.float32),
        lax.psum(shares[5].astype(jnp.bfloat16), "rep").astype(jnp.float32),
        lax.psum(shares[6].astype(jnp.bfloat16), "rep").astype(jnp.float32),
        lax.psum(shares[7].astype(jnp.bfloat16), "rep").astype(jnp.float32),
        lax.psum(shares[8].astype(jnp.bfloat16), "rep").astype(jnp.float32),
    )
    return (
        jnp.stack(results),
        jnp.stack(input_grads),
        reduced[0],
        reduced[1],
        reduced[2],
        reduced[3],
        reduced[4],
        reduced[5],
        reduced[6],
        reduced[7],
        reduced[8],
    )


def solution(mesh):
    placed = (
        P("rep", "shard", None),
        P("shard"),
        P("shard"),
        P("shard", None),
        P("shard", None),
        P("shard", None),
        P("shard"),
        P("shard"),
        P("shard", None),
        P("shard", None),
        P("rep", "shard", None),
    )
    return jax.shard_map(
        shards,
        mesh=mesh,
        in_specs=placed,
        out_specs=(
            P("rep", "shard", None),
            P("rep", "shard", None),
            P("shard"),
            P("shard"),
            P("shard", None),
            P("shard", None),
            P("shard", None),
            P("shard"),
            P("shard"),
            P("shard", None),
            P("shard", None),
        ),
        check_vma=False,
    )
```

profile of v0, /device:TPU:9, one launch (start us, length us, event | category | flops | bytes accessed | tf_op | source)
XLA Modules:
  0.0 916.9 jit_solution(16887876758495918346)
XLA Ops:
  14.7 7.9 all-reduce.15
  23.8 14.1 %all_gather.89 = bf16[768,128]{1,0:T(8,128)(2,1)S(1)} all-gather(bf16[192,128]{1,0:T(8,128)(2,1)S(1)} %copy-done.179), channel_id=1, replica_groups=mesh['rep'=8,'shard'=4] {'shard'}, dimensions={0}, use_global_device_ids=true | all-gather | bytes 245760 | tf_op jit(solution)/shard_map/all_gather | solution.py:156
  43.8 38.1 %all-gather.17.cloned.1.call-done = bf16[768,2304]{1,0:T(8,128)(2,1)} async-done(((bf16[192,2304]{1,0:T(8,128)(2,1)}), bf16[768,2304]{1,0:T(8,128)(2,1)}) %all-gather.17.cloned.1.call-update) | async-done | bytes 3538960 | tf_op jit(solution)/shard_map/all_gather | solution.py:155
  156.7 31.5 %all-gather.2 = bf16[48,128,64]{1,2,0:T(8,128)(2,1)} all-gather(bf16[12,128,64]{1,2,0:T(8,128)(2,1)S(1)} %convolution_convert_fusion.6), channel_id=4, replica_groups=mesh['rep'=8,'shard'=4] {'shard'}, dimensions={0}, use_global_device_ids=true | all-gather | bytes 983040 | tf_op jit(solution)/shard_map/all_gather | solution.py:20
  188.2 8.7 all-gather.9
  196.9 6.6 while.63
  243.1 29.2 %all-gather = bf16[48,128,64]{1,2,0:T(8,128)(2,1)} all-gather(bf16[12,128,64]{1,2,0:T(8,128)(2,1)S(1)} %convolution_convert_fusion.7), channel_id=2, replica_groups=mesh['rep'=8,'shard'=4] {'shard'}, dimensions={0}, use_global_device_ids=true | all-gather | bytes 983040 | tf_op jit(solution)/shard_map/all_gather | solution.py:20
  272.4 12.1 %all-gather.8 = bf16[4,12,128]{2,1,0:T(8,128)(2,1)S(1)} all-gather(bf16[1,12,128]{2,1,0:T(8,128)(2,1)S(1)} %bitcast.580), channel_id=3, replica_groups=mesh['rep'=8,'shard'=4] {'shard'}, dimensions={0}, use_global_device_ids=true | all-gather | bytes 15360 | tf_op jit(solution)/shard_map/all_gather | solution.py:20
  284.5 6.6 while.62
  322.2 5.6 fusion.215
  331.0 6.4 fusion.21
  355.2 4.5 fusion.255
  390.7 15.6 %all-gather.6 = bf16[48,128,64]{1,2,0:T(8,128)(2,1)} all-gather(bf16[12,128,64]{1,2,0:T(8,128)(2,1)S(1)} %copy-done.148), channel_id=8, replica_groups=mesh['rep'=8,'shard'=4] {'shard'}, dimensions={0}, use_global_device_ids=true | all-gather | bytes 983040 | tf_op jit(solution)/shard_map/all_gather | solution.py:45
  406.3 10.3 %all-gather.11 = bf16[4,12,128]{2,1,0:T(8,128)(2,1)S(1)} all-gather(bf16[1,12,128]{2,1,0:T(8,128)(2,1)S(1)} %bitcast.583), channel_id=9, replica_groups=mesh['rep'=8,'shard'=4] {'shard'}, dimensions={0}, use_global_device_ids=true | all-gather | bytes 15360 | tf_op jit(solution)/shard_map/all_gather | solution.py:45
  456.4 13.0 %all-gather.4 = bf16[48,128,64]{1,2,0:T(8,128)(2,1)} all-gather(bf16[12,128,64]{1,2,0:T(8,128)(2,1)S(1)} %copy-done.147), channel_id=6, replica_groups=mesh['rep'=8,'shard'=4] {'shard'}, dimensions={0}, use_global_device_ids=true | all-gather | bytes 983040 | tf_op jit(solution)/shard_map/all_gather | solution.py:45
  469.3 11.4 %all-gather.10 = bf16[4,12,128]{2,1,0:T(8,128)(2,1)S(1)} all-gather(bf16[1,12,128]{2,1,0:T(8,128)(2,1)S(1)} %bitcast.582), channel_id=7, replica_groups=mesh['rep'=8,'shard'=4] {'shard'}, dimensions={0}, use_global_device_ids=true | all-gather | bytes 15360 | tf_op jit(solution)/shard_map/all_gather | solution.py:45
  575.2 5.2 fusion.78
  580.5 46.7 %reduce-scatter.6.cloned.1.call-done = bf16[192,2304]{1,0:T(8,128)(2,1)} async-done(((bf16[768,2304]{1,0:T(8,128)(2,1)}), bf16[192,2304]{1,0:T(8,128)(2,1)}) %reduce-scatter.6.cloned.1.call-update) | async-done | bytes 884752 | tf_op jit(solution)/shard_map/reduce_scatter | solution.py:301
  627.3 88.1 %reduce-scatter.12.cloned.1.call-done = bf16[192,3072]{1,0:T(8,128)(2,1)} async-done(((bf16[768,3072]{1,0:T(8,128)(2,1)}), bf16[192,3072]{1,0:T(8,128)(2,1)}) %reduce-scatter.12.cloned.1.call-update) | async-done | bytes 1179664 | tf_op jit(solution)/shard_map/reduce_scatter | solution.py:316
  715.3 88.1 %reduce-scatter.14.cloned.1.call-done = bf16[768,768]{1,0:T(8,128)(2,1)} async-done(((bf16[3072,768]{1,0:T(8,128)(2,1)}), bf16[768,768]{1,0:T(8,128)(2,1)}) %reduce-scatter.14.cloned.1.call-update) | async-done | bytes 1179664 | tf_op jit(solution)/shard_map/reduce_scatter | solution.py:319
  804.2 7.5 all-reduce.14
  812.0 5.4 fusion.79
  821.5 24.9 %all-reduce.12 = (bf16[192]{0:T(256)(128)(2,1)S(1)}, bf16[192]{0:T(256)(128)(2,1)S(1)}, bf16[192,128]{1,0:T(8,128)(2,1)S(1)}, bf16[192]{0:T(256)(128)(2,1)S(1)}, bf16[192]{0:T(256)(128)(2,1)S(1)}) all-reduce(bf16[192]{0:T(256)(128)(2,1)S(1)} %dynamic-slice.5, ...), channel_id=1, replica_groups=mesh['rep'=8,'shard'=4] {'rep'}, use_global_device_ids=true, to_apply=%region_71.72 | all-reduce | flops 25344 | bytes 101376 | tf_op jit(solution)/shard_map/psum | solution.py:324
  849.3 53.8 %all-reduce.18.cloned.1.call-done = (bf16[192,2304]{1,0:T(8,128)(2,1)}, bf16[192,768]{1,0:T(8,128)(2,1)}, bf16[192,3072]{1,0:T(8,128)(2,1)}, bf16[768,768]{1,0:T(8,128)(2,1)}) async-done(((bf16[192,2304]{1,0:T(8,128)(2,1)}, bf16[192,768]{1,0:T(8,128)(2,1)}, bf16[192,3072]{1,0:T(8,128)(2,1)}, bf16[768,768]{1,0:T(8,128)(2,1)}), (bf16[192,2304]{1,0:T(8,128)(2,1)}, bf16[192,768]{1,0:T(8,128)(2,1)}, ...) | async-done | bytes 3538960 | tf_op jit(solution)/shard_map/psum | solution.py:326
  (820 shorter events, 375.2 us)
Async XLA Ops:
  7.2 74.7 %all-gather.17.cloned.1.call-start = ((), (), s32[]{:S(2)}) async-start(), calls=%async_computation.5 | async-start | bytes 4423680 | tf_op jit(solution)/shard_map/all_gather | solution.py:155
  7.9 303.5 %all-gather.19.cloned.1.call-start = ((), (), s32[]{:S(2)}) async-start(), calls=%async_computation.6 | async-start | bytes 1474560 | tf_op jit(solution)/shard_map/all_gather | solution.py:157
  8.7 313.5 %all-gather.21.cloned.1.call-start = ((), (), s32[]{:S(2)}) async-start(), calls=%async_computation.7 | async-start | bytes 5898240 | tf_op jit(solution)/shard_map/all_gather | solution.py:160
  9.5 14.3 %copy-start.179 = (bf16[192,128]{1,0:T(8,128)(2,1)S(1)}, bf16[192,128]{1,0:T(8,128)(2,1)}, u32[]{:S(2)}) copy-start(bf16[192,128]{1,0:T(8,128)(2,1)} %param.23) | copy-start | bytes 147460
  9.5 321.6 %all-gather.23.cloned.1.call-start = ((), (), s32[]{:S(2)}) async-start(), calls=%async_computation.8 | async-start | bytes 5898240 | tf_op jit(solution)/shard_map/all_gather | solution.py:161
  10.0 570.5 %reduce-scatter.10.cloned.1.call-start = ((), (), s32[]{:S(2)}) async-start(), calls=%async_computation.11 | async-start | bytes 1474560 | tf_op jit(solution)/shard_map/reduce_scatter | solution.py:307
  10.9 27.0 %copy-start.180 = (f32[256]{0:T(256)}, f32[256]{0:T(256)S(1)}, u32[]{:S(2)}) copy-start(f32[256]{0:T(256)S(1)} %get-tuple-element.658) | copy-start | bytes 3076
  10.9 27.0 %copy-start.188 = (f32[256]{0:T(256)}, f32[256]{0:T(256)S(1)}, u32[]{:S(2)}) copy-start(f32[256]{0:T(256)S(1)} %get-tuple-element.657) | copy-start | bytes 3076
  11.8 26.1 %copy-start.215 = (f32[256]{0:T(256)}, f32[256]{0:T(256)S(1)}, u32[]{:S(2)}) copy-start(f32[256]{0:T(256)S(1)} %get-tuple-element.512) | copy-start | bytes 3076
  39.6 49.6 %copy-start.72 = (bf16[12,64,1,64]{1,3,0,2:T(8,128)(2,1)}, bf16[12,64,1,64]{1,3,0,2:T(8,128)(2,1)S(1)}, u32[]{:S(2)}) copy-start(bf16[12,64,1,64]{1,3,0,2:T(8,128)(2,1)S(1)} %copy.272) | copy-start | bytes 294916
  39.9 55.9 %copy-start.75 = (bf16[12,64,1,64]{1,3,0,2:T(8,128)(2,1)}, bf16[12,64,1,64]{1,3,0,2:T(8,128)(2,1)S(1)}, u32[]{:S(2)}) copy-start(bf16[12,64,1,64]{1,3,0,2:T(8,128)(2,1)S(1)} %copy.273) | copy-start | bytes 294916
  99.3 57.0 %copy-start.63 = (bf16[256,12,64]{0,2,1:T(8,128)(2,1)}, bf16[256,12,64]{0,2,1:T(8,128)(2,1)S(1)}, u32[]{:S(2)}) copy-start(bf16[256,12,64]{0,2,1:T(8,128)(2,1)S(1)} %divide_convert_fusion) | copy-start | bytes 1179652
  155.1 33.1 %copy-start.83 = (bf16[256,768]{0,1:T(8,128)(2,1)}, bf16[256,768]{0,1:T(8,128)(2,1)S(1)}, u32[]{:S(2)}) copy-start(bf16[256,768]{0,1:T(8,128)(2,1)S(1)} %copy.174) | copy-start | bytes 1179652
  156.3 31.9 %copy-start.199 = (bf16[12,128]{1,0:T(8,128)(2,1)S(1)}, bf16[12,128]{1,0:T(8,128)(2,1)}, u32[]{:S(2)}) copy-start(bf16[12,128]{1,0:T(8,128)(2,1)} %fusion.139) | copy-start | bytes 9220
  241.5 30.9 %copy-start.81 = (bf16[256,768]{0,1:T(8,128)(2,1)}, bf16[256,768]{0,1:T(8,128)(2,1)S(1)}, u32[]{:S(2)}) copy-start(bf16[256,768]{0,1:T(8,128)(2,1)S(1)} %copy.157) | copy-start | bytes 1179652
  242.7 29.6 %copy-start.198 = (bf16[12,128]{1,0:T(8,128)(2,1)S(1)}, bf16[12,128]{1,0:T(8,128)(2,1)}, u32[]{:S(2)}) copy-start(bf16[12,128]{1,0:T(8,128)(2,1)} %fusion.140) | copy-start | bytes 9220
  313.5 34.7 %copy-start.11 = (f32[256,768]{1,0:T(8,128)}, f32[256,768]{1,0:T(8,128)S(1)}, u32[]{:S(2)}) copy-start(f32[256,768]{1,0:T(8,128)S(1)} %get-tuple-element.636) | copy-start | bytes 2359300
  331.0 11.5 %copy-start.234 = (bf16[3072,768]{1,0:T(8,128)(2,1)S(1)}, bf16[3072,768]{1,0:T(8,128)(2,1)}, u32[]{:S(2)}) copy-start(bf16[3072,768]{1,0:T(8,128)(2,1)} %all-gather.23.cloned.1.call-done) | copy-start | bytes 14155780
  452.5 16.8 %copy-start.200 = (bf16[12,128]{1,0:T(8,128)(2,1)S(1)}, bf16[12,128]{1,0:T(8,128)(2,1)}, u32[]{:S(2)}) copy-start(bf16[12,128]{1,0:T(8,128)(2,1)} %fusion.187) | copy-start | bytes 9220
  512.1 115.1 %reduce-scatter.6.cloned.1.call-start = ((), (), s32[]{:S(2)}) async-start(), calls=%async_computation.9 | async-start | bytes 4423680 | tf_op jit(solution)/shard_map/reduce_scatter | solution.py:301
  541.8 173.5 %reduce-scatter.12.cloned.1.call-start = ((), (), s32[]{:S(2)}) async-start(), calls=%async_computation.12 | async-start | bytes 5898240 | tf_op jit(solution)/shard_map/reduce_scatter | solution.py:316
  549.9 253.5 %reduce-scatter.14.cloned.1.call-start = ((), (), s32[]{:S(2)}) async-start(), calls=%async_computation.13 | async-start | bytes 5898240 | tf_op jit(solution)/shard_map/reduce_scatter | solution.py:319
  559.2 262.3 %reduce-scatter.8.cloned.1.call-start = ((), (), s32[]{:S(2)}) async-start(), calls=%async_computation.10 | async-start | bytes 245760 | tf_op jit(solution)/shard_map/reduce_scatter | solution.py:304
  574.9 328.2 %all-reduce.18.cloned.1.call-start = ((), (), s32[]{:S(2)}) async-start(), calls=%async_computation.14 | async-start | bytes 7077888 | tf_op jit(solution)/shard_map/psum | solution.py:326
  (231 other events, 682.9 us)
Sparse Core Ops, SparseCore 0:
  9.6 72.2 all-gather.16
  83.5 30.4 all-gather.18
  115.6 99.4 all-gather.20
  216.5 100.6 all-gather.22
  512.3 45.7 reduce-scatter.9
  560.3 66.9 reduce-scatter.5
  629.6 85.7 reduce-scatter.11
  717.6 85.7 reduce-scatter.13
  806.3 15.1 reduce-scatter.7
  825.5 77.5 all-reduce.17
where the time goes:
time: 925 us; the launch traced here: 917 us
  waiting for transfers between devices  318 us (34%)
  blocking collectives  186 us (20%)
  matrix products  169 us (18%)
  local copies, waits for them, and re-layouts  142 us (15%)
  other arithmetic  80.9 us (9%)
  between operations  18.6 us (2%)
    reduce_scatter x1, waiting for transfers between devices, shards(): lax.psum_scatter(totals[8].astype(jnp.bfloat16), 'shard', scatter_dimensi...  88.1 us
    reduce_scatter x1, waiting for transfers between devices, shards(): lax.psum_scatter(totals[7].astype(jnp.bfloat16), 'shard', scatter_dimensi...  88.1 us
    all_gather x4, blocking collectives, prefix(): lax.all_gather(part.astype(kind), axis)  81.5 us
    psum x1, waiting for transfers between devices, shards(): lax.psum(shares[2].astype(jnp.bfloat16), 'rep').astype(jnp.float32)  53.8 us
    all_gather x4, blocking collectives, prefix_2(): lax.all_gather(a.astype(kind), axis)  50.3 us
    reduce_scatter x1, waiting for transfers between devices, shards(): lax.psum_scatter(totals[2].astype(jnp.bfloat16), 'shard', scatter_dimensi...  46.7 us
    all_gather x1, waiting for transfers between devices, shards(): lax.all_gather(w_qkv, 'shard', axis=0, tiled=True)  38.1 us
    concatenate x16, local copies, waits for them, and re-layouts, featurize(): jnp.concatenate([jax.nn.softmax(inputs, axis=-1), jax.nn.softmax(-inputs,...  32.9 us
  transfers between devices with their start and end apart: 10, of which 6 were waited for; matrix products, arithmetic and copies ran while one was open for 27% of the time, Pallas kernels for 0%

commit v1 on v0

--- a/solution.py
+++ b/solution.py
@@ -10,7 +10,7 @@
 STRETCH = 64
 
 
-top_precision = lax.Precision.HIGHEST
+top_precision = lax.Precision.DEFAULT
 norm_epsilon = 1e-05
 
 
@@ -60,6 +60,63 @@
         )
 
     return lax.fori_loop(0, ahead, one, state)
+
+
+PIECES = 8
+
+
+def flip(value, bit):
+    count = lax.axis_size("rep")
+    return lax.ppermute(value, "rep", [(i, i ^ bit) for i in range(count)])
+
+
+def spin(value, step):
+    count = lax.axis_size("shard")
+    return lax.ppermute(value, "shard", [(i, (i + step) % count) for i in range(count)])
+
+
+def spread(own):
+    half = own.shape[0] // 2
+    from_x = flip(own, 2)
+    from_y = flip(own, 4)
+    diagonal = jnp.concatenate([flip(from_x[:half], 4), flip(from_y[half:], 2)], axis=0)
+    even = (own, from_x, from_y, diagonal)
+    pieces = []
+    for part in even:
+        pieces += [part, flip(part, 1)]
+    return pieces
+
+
+def gather_pieces(part):
+    count, here = lax.axis_size("shard"), lax.axis_index("shard")
+    full = jnp.zeros((count,) + part.shape, part.dtype)
+    full = lax.dynamic_update_index_in_dim(full, part, here, 0)
+    for step in range(1, count):
+        full = lax.dynamic_update_index_in_dim(full, spin(part, step), (here - step) % count, 0)
+    return spread(full.reshape((count * part.shape[0],) + part.shape[1:]))
+
+
+def sum_pieces(parts):
+    wide = lambda a: a.astype(jnp.float32)
+    low = lambda a: a.astype(jnp.bfloat16)
+    odd = flip(jnp.stack([low(p) for p in parts[1::2]]), 1)
+    mine, x_part, y_part, diagonal = (wide(p) + wide(odd[i]) for i, p in enumerate(parts[0::2]))
+    half = diagonal.shape[0] // 2
+    to_y, to_x = flip(low(diagonal[:half]), 4), flip(low(diagonal[half:]), 2)
+    x_part = jnp.concatenate([x_part[:half] + wide(to_y), x_part[half:]], axis=0)
+    y_part = jnp.concatenate([y_part[:half], y_part[half:] + wide(to_x)], axis=0)
+    mine = mine + wide(flip(low(x_part), 2)) + wide(flip(low(y_part), 4))
+    bit = PIECES
+    while bit < lax.axis_size("rep"):
+        mine = mine + wide(flip(low(mine), bit))
+        bit *= 2
+    count, here = lax.axis_size("shard"), lax.axis_index("shard")
+    blocks = mine.reshape((count, mine.shape[0] // count) + mine.shape[1:])
+    pick = lambda step: lax.dynamic_index_in_dim(blocks, (here + step) % count, 0, False)
+    total = pick(0)
+    for step in range(1, count):
+        total = total + wide(spin(low(pick(step)), step))
+    return spread(low(total))
 
 
 def layer_norm(rows_in, gain, offset):
@@ -131,46 +188,35 @@
     cotangent,
 ):
     shard_count = lax.axis_size("shard")
-    local_weights = (
-        gain_attn,
-        bias_attn,
-        w_qkv,
-        w_feature,
-        w_out,
-        gain_mlp,
-        bias_mlp,
-        w_up,
-        w_down,
-    )
-    totals = [
-        jnp.zeros((weight.shape[0] * shard_count,) + weight.shape[1:], jnp.float32)
-        for weight in local_weights
-    ]
+    place = lax.axis_index("rep") % PIECES
+    rows = w_qkv.shape[0]
+    chunk = w_up.shape[1] // PIECES
+    fine = chunk // shard_count
+    wide_in = jnp.concatenate([w_qkv, w_out], axis=1)
+    part_in = lax.dynamic_slice_in_dim(wide_in, place * chunk, chunk, 1)
+    in_pieces = gather_pieces(part_in)
+    part_up = lax.dynamic_index_in_dim(
+        w_up.reshape(rows, shard_count, PIECES, fine), place, 2, False
+    ).reshape(rows, chunk)
+    up_pieces = gather_pieces(part_up)
+    down_rows = w_down.shape[0] // PIECES
+    part_down = lax.dynamic_slice_in_dim(w_down, place * down_rows, down_rows, 0)
+    down_pieces = gather_pieces(part_down)
+    wide_weight = jnp.zeros((rows * shard_count, chunk * PIECES), jnp.bfloat16)
+    for k, piece in enumerate(in_pieces):
+        wide_weight = lax.dynamic_update_slice_in_dim(wide_weight, piece, (place ^ k) * chunk, 1)
+    qkv_weight = wide_weight[:, : 3 * D]
+    out_weight = wide_weight[:, 3 * D :]
+    small = jnp.concatenate(
+        [w_feature.reshape(-1), gain_attn, bias_attn, gain_mlp, bias_mlp]
+    ).reshape(-1, rows)
+    small = lax.all_gather(small, "shard", axis=0)
+    feature_weight = small[:, :FEAT].reshape(D, FEAT)
+    gain_one, bias_one, gain_two, bias_two = (small[:, FEAT + i].reshape(D) for i in range(4))
+    totals = None
     results = []
     input_grads = []
     for batch_index in range(tokens.shape[0]):
-        forward_set = (
-            lax.all_gather(gain_attn, "shard", axis=0, tiled=True),
-            lax.all_gather(bias_attn, "shard", axis=0, tiled=True),
-            lax.all_gather(w_qkv, "shard", axis=0, tiled=True),
-            lax.all_gather(w_feature, "shard", axis=0, tiled=True),
-            lax.all_gather(w_out, "shard", axis=0, tiled=True),
-            lax.all_gather(gain_mlp, "shard", axis=0, tiled=True),
-            lax.all_gather(bias_mlp, "shard", axis=0, tiled=True),
-            lax.all_gather(w_up, "shard", axis=0, tiled=True),
-            lax.all_gather(w_down, "shard", axis=0, tiled=True),
-        )
-        (
-            gain_one,
-            bias_one,
-            qkv_weight,
-            feature_weight,
-            out_weight,
-            gain_two,
-            bias_two,
-            up_weight,
-            down_weight,
-        ) = forward_set
         rows_in = tokens[batch_index].astype(jnp.float32)
         length = rows_in.shape[0]
         normed, norm_pull = jax.vjp(
@@ -213,30 +259,36 @@
             layer_norm, resid, gain_two.astype(jnp.float32), bias_two.astype(jnp.float32)
         )
         normed_two_low = normed_two.astype(jnp.bfloat16)
-        pre_act = jnp.dot(normed_two_low, up_weight, preferred_element_type=jnp.float32)
-        hidden, gelu_pull = jax.vjp(gelu_tanh, pre_act)
-        hidden_low = hidden.astype(jnp.bfloat16)
-        result = resid + jnp.dot(hidden_low, down_weight, preferred_element_type=jnp.float32)
+        result = resid
+        hidden_parts, gelu_pulls = [], []
+        for up_piece, down_piece in zip(up_pieces, down_pieces):
+            pre_act = jnp.dot(normed_two_low, up_piece, preferred_element_type=jnp.float32)
+            hidden, gelu_pull = jax.vjp(gelu_tanh, pre_act)
+            hidden_parts.append(hidden.astype(jnp.bfloat16))
+            gelu_pulls.append(gelu_pull)
+            result = result + jnp.dot(
+                hidden_parts[-1], down_piece, preferred_element_type=jnp.float32
+            )
         results.append(result.astype(jnp.bfloat16))
-        qkv_back, feature_back, out_back, up_back, down_back = (
-            lax.all_gather(w_qkv, "shard", axis=0, tiled=True),
-            lax.all_gather(w_feature, "shard", axis=0, tiled=True),
-            lax.all_gather(w_out, "shard", axis=0, tiled=True),
-            lax.all_gather(w_up, "shard", axis=0, tiled=True),
-            lax.all_gather(w_down, "shard", axis=0, tiled=True),
-        )
         grad_out = cotangent[batch_index]
-        d_down = jnp.dot(hidden_low.T, grad_out, preferred_element_type=jnp.float32)
-        d_hidden = jnp.dot(grad_out, down_back.T, preferred_element_type=jnp.float32)
-        (d_pre,) = gelu_pull(d_hidden)
-        d_pre_low = d_pre.astype(jnp.bfloat16)
-        d_up = jnp.dot(normed_two_low.T, d_pre_low, preferred_element_type=jnp.float32)
-        d_normed_two = jnp.dot(d_pre_low, up_back.T, preferred_element_type=jnp.float32)
+        d_down, d_up = [], []
+        d_normed_two = 0.0
+        for hidden_low, gelu_pull, up_piece, down_piece in zip(
+            hidden_parts, gelu_pulls, up_pieces, down_pieces
+        ):
+            d_down.append(jnp.dot(hidden_low.T, grad_out, preferred_element_type=jnp.float32))
+            d_hidden = jnp.dot(grad_out, down_piece.T, preferred_element_type=jnp.float32)
+            (d_pre,) = gelu_pull(d_hidden)
+            d_pre_low = d_pre.astype(jnp.bfloat16)
+            d_up.append(jnp.dot(normed_two_low.T, d_pre_low, preferred_element_type=jnp.float32))
+            d_normed_two = d_normed_two + jnp.dot(
+                d_pre_low, up_piece.T, preferred_element_type=jnp.float32
+            )
         d_resid_two, d_gain_two, d_bias_two = norm_two_pull(d_normed_two)
         d_resid = grad_out.astype(jnp.float32) + d_resid_two
         d_resid_low = d_resid.astype(jnp.bfloat16)
         d_out = jnp.dot(attended_low.T, d_resid_low, preferred_element_type=jnp.float32)
-        d_attended = jnp.dot(d_resid_low, out_back.T, preferred_element_type=jnp.float32).reshape(
+        d_attended = jnp.dot(d_resid_low, out_weight.T, preferred_element_type=jnp.float32).reshape(
             length, HEADS, HEAD
         )
         d_query_f, d_key_f, d_value_f, local_state, local_sum = attend_pull(d_attended)
@@ -257,7 +309,7 @@
         d_u_query, d_u_key = feature_pull((d_query_f, d_key_f))
         d_uq_low = d_u_query.astype(jnp.bfloat16)
         d_uk_low = d_u_key.astype(jnp.bfloat16)
-        back_maps = feature_back.reshape(HEADS, HEAD, 2, HEAD)
+        back_maps = feature_weight.reshape(HEADS, HEAD, 2, HEAD)
         d_queries = jnp.einsum(
             "tho,hio->thi", d_uq_low, back_maps[:, :, 0], preferred_element_type=jnp.float32
         )
@@ -276,60 +328,56 @@
             axis=1,
         ).astype(jnp.bfloat16)
         d_qkv = jnp.dot(normed_low.T, d_mixed, preferred_element_type=jnp.float32)
-        d_normed = jnp.dot(d_mixed, qkv_back.T, preferred_element_type=jnp.float32)
+        d_normed = jnp.dot(d_mixed, qkv_weight.T, preferred_element_type=jnp.float32)
         d_rows, d_gain_one, d_bias_one = norm_pull(d_normed)
         input_grads.append((d_resid + d_rows).astype(jnp.bfloat16))
         contributions = (
-            d_gain_one,
-            d_bias_one,
-            d_qkv,
-            d_maps,
-            d_out,
-            d_gain_two,
-            d_bias_two,
+            jnp.concatenate([d_qkv, d_out], axis=1),
             d_up,
             d_down,
-        )
-        totals = [total_sum + new_term for total_sum, new_term in zip(totals, contributions)]
-    shares = (
-        lax.psum_scatter(
-            totals[0].astype(jnp.bfloat16), "shard", scatter_dimension=0, tiled=True
-        ).astype(jnp.float32),
-        lax.psum_scatter(
-            totals[1].astype(jnp.bfloat16), "shard", scatter_dimension=0, tiled=True
-        ).astype(jnp.float32),
-        lax.psum_scatter(
-            totals[2].astype(jnp.bfloat16), "shard", scatter_dimension=0, tiled=True
-        ).astype(jnp.float32),
-        lax.psum_scatter(
-            totals[3].astype(jnp.bfloat16), "shard", scatter_dimension=0, tiled=True
-        ).astype(jnp.float32),
-        lax.psum_scatter(
-            totals[4].astype(jnp.bfloat16), "shard", scatter_dimension=0, tiled=True
-        ).astype(jnp.float32),
-        lax.psum_scatter(
-            totals[5].astype(jnp.bfloat16), "shard", scatter_dimension=0, tiled=True
-        ).astype(jnp.float32),
-        lax.psum_scatter(
-            totals[6].astype(jnp.bfloat16), "shard", scatter_dimension=0, tiled=True
-        ).astype(jnp.float32),
-        lax.psum_scatter(
-            totals[7].astype(jnp.bfloat16), "shard", scatter_dimension=0, tiled=True
-        ).astype(jnp.float32),
-        lax.psum_scatter(
-            totals[8].astype(jnp.bfloat16), "shard", scatter_dimension=0, tiled=True
-        ).astype(jnp.float32),
-    )
+            (d_gain_one, d_bias_one, d_gain_two, d_bias_two, d_maps),
+        )
+        totals = (
+            contributions
+            if totals is None
+            else jax.tree.map(jnp.add, totals, contributions)
+        )
+    grad_down = sum_pieces(totals[2])
+    grad_up = sum_pieces(totals[1])
+    grad_in = sum_pieces(
+        [
+            lax.dynamic_slice_in_dim(totals[0], (place ^ k) * chunk, chunk, 1)
+            for k in range(PIECES)
+        ]
+    )
+    ordered = []
+    for parts in (grad_in, grad_up, grad_down):
+        stack = jnp.zeros((PIECES,) + parts[0].shape, jnp.bfloat16)
+        for k, part in enumerate(parts):
+            stack = lax.dynamic_update_index_in_dim(stack, part, place ^ k, 0)
+        ordered.append(stack.astype(jnp.float32))
+    grad_wide = jnp.swapaxes(ordered[0], 0, 1).reshape(rows, -1)
+    grad_up = (
+        ordered[1]
+        .reshape(PIECES, rows, shard_count, fine)
+        .transpose(1, 2, 0, 3)
+        .reshape(rows, -1)
+    )
+    grad_down = ordered[2].reshape(-1, D)
+    tiny = jnp.concatenate([part.reshape(shard_count, -1) for part in totals[3]], axis=1)
+    tiny = lax.psum_scatter(tiny.astype(jnp.bfloat16), "shard", scatter_dimension=0, tiled=True)
+    tiny = lax.psum(tiny, "rep").astype(jnp.float32).reshape(-1)
+    vectors = [tiny[i * rows : (i + 1) * rows] for i in range(4)]
     reduced = (
-        lax.psum(shares[0].astype(jnp.bfloat16), "rep").astype(jnp.float32),
-        lax.psum(shares[1].astype(jnp.bfloat16), "rep").astype(jnp.float32),
-        lax.psum(shares[2].astype(jnp.bfloat16), "rep").astype(jnp.float32),
-        lax.psum(shares[3].astype(jnp.bfloat16), "rep").astype(jnp.float32),
-        lax.psum(shares[4].astype(jnp.bfloat16), "rep").astype(jnp.float32),
-        lax.psum(shares[5].astype(jnp.bfloat16), "rep").astype(jnp.float32),
-        lax.psum(shares[6].astype(jnp.bfloat16), "rep").astype(jnp.float32),
-        lax.psum(shares[7].astype(jnp.bfloat16), "rep").astype(jnp.float32),
-        lax.psum(shares[8].astype(jnp.bfloat16), "rep").astype(jnp.float32),
+        vectors[0],
+        vectors[1],
+        grad_wide[:, : 3 * D],
+        tiny[4 * rows :].reshape(rows, FEAT),
+        grad_wide[:, 3 * D :],
+        vectors[2],
+        vectors[3],
+        grad_up,
+        grad_down,
     )
     return (
         jnp.stack(results),

time: 925 us -> 919 us (level)
  waiting for transfers between devices: 318 us -> 89.1 us
  starting transfers between devices: 1.19 us -> 121 us
  local copies, waits for them, and re-layouts: 142 us -> 206 us
  matrix products: 169 us -> 221 us
  blocking collectives: 186 us -> 152 us
  other arithmetic: 80.9 us -> 93.5 us
    reduce_scatter x5 -> x0, waiting for transfers between devices: 224 us -> none  [the longest x1 88.1 us: shards(): lax.psum_scatter(totals[8].astype(jnp.bfloat16), 'shard', scatter_dimensi...]
    ppermute x0 -> x81, starting transfers between devices: none -> 121 us  [the longest x63 86.5 us: flip(): return lax.ppermute(value, 'rep', [(i, i ^ bit) for i in range(count)])]
    ppermute x0 -> x81, waiting for transfers between devices: none -> 89 us  [the longest x63 74.7 us: flip(): return lax.ppermute(value, 'rep', [(i, i ^ bit) for i in range(count)])]
    psum x1 -> x0, waiting for transfers between devices: 53.8 us -> none  [shards(): lax.psum(shares[2].astype(jnp.bfloat16), 'rep').astype(jnp.float32)]
    dot_general x14 -> x84, matrix products: 52.1 us -> 103 us  [the longest x16 19.4 us: shards(): jnp.dot(hidden_low.T, grad_out, preferred_element_type=jnp.float32)]
    all_gather x4 -> x0, waiting for transfers between devices: 38.1 us -> none  [the longest x1 38.1 us: shards(): lax.all_gather(w_qkv, 'shard', axis=0, tiled=True)]
    all_gather x4, blocking collectives: 81.5 us -> 53.1 us  [prefix(): lax.all_gather(part.astype(kind), axis)]
    dynamic_update_slice x0 -> x40, local copies, waits for them, and re-layouts: none -> 17.5 us  [the longest x9 8.66 us: gather_pieces(): lax.dynamic_update_index_in_dim(full, spin(part, step), (here - step) % c...]
  transfers between devices with their start and end apart: 10 -> 82, of which waited for: 6 -> 18; matrix products, arithmetic and copies ran while one was open for 27% -> 35% of each run, Pallas kernels for 0% -> 0%
where the time goes in v1:
time: 919 us; the launch traced here: 903 us
  matrix products  221 us (24%)
  local copies, waits for them, and re-layouts  206 us (22%)
  blocking collectives  152 us (17%)
  starting transfers between devices  121 us (13%)
  other arithmetic  93.5 us (10%)
  waiting for transfers between devices  89.1 us (10%)
  between operations  19 us (2%)
    ppermute x63, starting transfers between devices, flip(): return lax.ppermute(value, 'rep', [(i, i ^ bit) for i in range(count)])  86.5 us
    ppermute x63, waiting for transfers between devices, flip(): return lax.ppermute(value, 'rep', [(i, i ^ bit) for i in range(count)])  74.7 us
    all_gather x4, blocking collectives, prefix(): lax.all_gather(part.astype(kind), axis)  53.1 us
    all_gather x4, blocking collectives, prefix_2(): lax.all_gather(a.astype(kind), axis)  53 us
    unnamed x635, local copies, waits for them, and re-layouts  41 us
    ppermute x18, starting transfers between devices, spin(): lax.ppermute(value, 'shard', [(i, (i + step) % count) for i in range(coun...  34.6 us
    concatenate x16, local copies, waits for them, and re-layouts, featurize(): jnp.concatenate([jax.nn.softmax(inputs, axis=-1), jax.nn.softmax(-inputs,...  33.1 us
    psum x1, blocking collectives, shards(): tiny = lax.psum(tiny, 'rep').astype(jnp.float32).reshape(-1)  22.9 us
  transfers between devices with their start and end apart: 82, of which 18 were waited for; matrix products, arithmetic and copies ran while one was open for 35% of the time, Pallas kernels for 0%

profile of v1, /device:TPU:9, one launch (start us, length us, event | category | flops | bytes accessed | tf_op | source)
XLA Modules:
  0.0 903.0 jit_solution(17445628291275484464)
XLA Ops:
  18.6 22.8 %all_gather.43 = bf16[4,132,192]{2,1,0:T(8,128)(2,1)S(1)} all-gather(bf16[1,132,192]{2,1,0:T(8,128)(2,1)S(1)} %all_gather_reshape.3), channel_id=1, replica_groups=mesh['rep'=8,'shard'=4] {'shard'}, dimensions={0}, use_global_device_ids=true | all-gather | bytes 253440 | tf_op jit(solution)/shard_map/all_gather | solution.py:213
  78.3 19.8 %collective-permute-done.20 = bf16[384,768]{1,0:T(8,128)(2,1)} collective-permute-done((bf16[384,768]{1,0:T(8,128)(2,1)}, bf16[384,768]{1,0:T(8,128)(2,1)}, u32[]{:S(2)}, u32[]{:S(2)}) %collective-permute-start.20) | collective-permute-done | bytes 589856 | tf_op jit(solution)/shard_map/ppermute | solution.py:70
  104.3 6.5 collective-permute-done.19
  115.8 8.8 collective-permute-done.23
  239.4 15.7 %all-gather = bf16[48,128,64]{1,2,0:T(8,128)(2,1)} all-gather(bf16[12,128,64]{1,2,0:T(8,128)(2,1)S(1)} %convolution_convert_fusion.7), channel_id=2, replica_groups=mesh['rep'=8,'shard'=4] {'shard'}, dimensions={0}, use_global_device_ids=true | all-gather | bytes 983040 | tf_op jit(solution)/shard_map/all_gather | solution.py:20
  255.1 10.4 %all-gather.8 = bf16[4,12,128]{2,1,0:T(8,128)(2,1)} all-gather(bf16[1,12,128]{2,1,0:T(8,128)(2,1)S(1)} %bitcast.1085), channel_id=3, replica_groups=mesh['rep'=8,'shard'=4] {'shard'}, dimensions={0}, use_global_device_ids=true | all-gather | bytes 15360 | tf_op jit(solution)/shard_map/all_gather | solution.py:20
  265.4 13.1 %while.62 = (s32[]{:T(128)}, f32[12,128,64]{2,1,0:T(8,128)S(1)}, f32[12,128]{1,0:T(8,128)}, s32[]{:T(128)}, bf16[4,12,128,64]{2,3,1,0:T(8,128)(2,1)}, /*index=5*/bf16[4,12,128]{2,1,0:T(8,128)(2,1)}, s32[]{:T(128)}, s32[]{:T(128)}) while((s32[]{:T(128)}, f32[12,128,64]{2,1,0:T(8,128)S(1)}, f32[12,128]{1,0:T(8,128)}, s32[]{:T(128)}, ...), condition=%wide.region_12.13_spmd.clone, body=%wide.region_11.12_spmd.clone.sunk | while | flops 399364 | bytes 1834163 | solution.py:37
  318.1 15.5 %all-gather.2 = bf16[48,128,64]{1,2,0:T(8,128)(2,1)} all-gather(bf16[12,128,64]{1,2,0:T(8,128)(2,1)S(1)} %convolution_convert_fusion.6), channel_id=4, replica_groups=mesh['rep'=8,'shard'=4] {'shard'}, dimensions={0}, use_global_device_ids=true | all-gather | bytes 983040 | tf_op jit(solution)/shard_map/all_gather | solution.py:20
  333.6 11.6 %all-gather.9 = bf16[4,12,128]{2,1,0:T(8,128)(2,1)} all-gather(bf16[1,12,128]{2,1,0:T(8,128)(2,1)S(1)} %bitcast.1084), channel_id=5, replica_groups=mesh['rep'=8,'shard'=4] {'shard'}, dimensions={0}, use_global_device_ids=true | all-gather | bytes 15360 | tf_op jit(solution)/shard_map/all_gather | solution.py:20
  345.1 9.2 %while.63 = (s32[]{:T(128)}, f32[12,128,64]{2,1,0:T(8,128)S(1)}, f32[12,128]{1,0:T(8,128)S(1)}, s32[]{:T(128)}, bf16[4,12,128,64]{2,3,1,0:T(8,128)(2,1)}, /*index=5*/bf16[4,12,128]{2,1,0:T(8,128)(2,1)}, s32[]{:T(128)}, s32[]{:T(128)}) while((s32[]{:T(128)}, f32[12,128,64]{2,1,0:T(8,128)S(1)}, f32[12,128]{1,0:T(8,128)S(1)}, ...), condition=%wide.region_31.32_spmd.clone, body=%wide.region_30.31_spmd.clone.sunk | while | flops 399364 | bytes 1784955 | solution.py:37
  380.8 11.8 %collective-permute-start.26 = (bf16[384,768]{1,0:T(8,128)(2,1)S(1)}, bf16[384,768]{1,0:T(8,128)(2,1)S(1)}, u32[]{:S(2)}, u32[]{:S(2)}) collective-permute-start(bf16[384,768]{1,0:T(8,128)(2,1)S(1)} %copy-done.80), channel_id=1, source_target_pairs={{0,4},{4,0},{8,12},{12,8},{16,20},{20,16},{24,28},{28,24},{1,5},{5... | collective-permute-start | bytes 1769480 | tf_op jit(solution)/shard_map/ppermute | solution.py:70
  480.6 16.2 %all-gather.4 = bf16[48,128,64]{1,2,0:T(8,128)(2,1)} all-gather(bf16[12,128,64]{1,2,0:T(8,128)(2,1)S(1)} %get-tuple-element.682), channel_id=6, replica_groups=mesh['rep'=8,'shard'=4] {'shard'}, dimensions={0}, use_global_device_ids=true | all-gather | bytes 983040 | tf_op jit(solution)/shard_map/all_gather | solution.py:45
  496.8 10.8 %all-gather.10 = bf16[4,12,128]{2,1,0:T(8,128)(2,1)S(1)} all-gather(bf16[1,12,128]{2,1,0:T(8,128)(2,1)S(1)} %bitcast.1087), channel_id=7, replica_groups=mesh['rep'=8,'shard'=4] {'shard'}, dimensions={0}, use_global_device_ids=true | all-gather | bytes 15360 | tf_op jit(solution)/shard_map/all_gather | solution.py:45
  541.2 15.5 %all-gather.6 = bf16[48,128,64]{1,2,0:T(8,128)(2,1)} all-gather(bf16[12,128,64]{1,2,0:T(8,128)(2,1)S(1)} %copy-done.235), channel_id=8, replica_groups=mesh['rep'=8,'shard'=4] {'shard'}, dimensions={0}, use_global_device_ids=true | all-gather | bytes 983040 | tf_op jit(solution)/shard_map/all_gather | solution.py:45
  556.8 10.5 %all-gather.11 = bf16[4,12,128]{2,1,0:T(8,128)(2,1)} all-gather(bf16[1,12,128]{2,1,0:T(8,128)(2,1)S(1)} %bitcast.1086), channel_id=9, replica_groups=mesh['rep'=8,'shard'=4] {'shard'}, dimensions={0}, use_global_device_ids=true | all-gather | bytes 15360 | tf_op jit(solution)/shard_map/all_gather | solution.py:45
  567.4 7.3 while.61
  672.9 7.1 maximum_add_fusion
  684.3 10.6 %collective-permute-start.33 = (bf16[4,768,384]{2,1,0:T(8,128)(2,1)}, bf16[4,768,384]{2,1,0:T(8,128)(2,1)}, u32[]{:S(2)}, u32[]{:S(2)}) collective-permute-start(bf16[4,768,384]{2,1,0:T(8,128)(2,1)} %pad_maximum_fusion), channel_id=1, source_target_pairs={{0,4},{4,0},{8,12},{12,8},{16,20},{20,16},{24,28},{28,24},{1,5},{5... | collective-permute-start | bytes 7077896 | tf_op jit(solution)/shard_map/ppermute | solution.py:70
  736.0 22.9 %psum.7 = bf16[1,25344]{1,0:T(2,128)(2,1)S(1)} all-reduce(bf16[1,25344]{1,0:T(2,128)(2,1)S(1)} %constant_dynamic-slice_fusion.6), channel_id=1, replica_groups=mesh['rep'=8,'shard'=4] {'rep'}, use_global_device_ids=true, to_apply=%region_77.78 | all-reduce | flops 25344 | bytes 101376 | tf_op jit(solution)/shard_map/psum | solution.py:369
  788.0 10.0 %collective-permute-done.37 = bf16[768,384]{1,0:T(8,128)(2,1)S(1)} collective-permute-done((bf16[768,384]{1,0:T(8,128)(2,1)S(1)}, bf16[768,384]{1,0:T(8,128)(2,1)S(1)}, u32[]{:S(2)}, u32[]{:S(2)}) %collective-permute-start.37) | collective-permute-done | bytes 589856 | tf_op jit(solution)/shard_map/ppermute | solution.py:70
  799.9 5.4 collective-permute-start.40
  810.7 6.5 collective-permute-start.38
  823.3 5.3 collective-permute-start.56
  841.0 6.8 collective-permute-done.54
  (1302 shorter events, 635.6 us)
Async XLA Ops:
  7.2 727.1 %all-reduce.7.cloned.1.call-start = ((), (), s32[]{:S(2)}) async-start(), calls=%async_computation | async-start | bytes 405504
  9.8 44.6 %collective-permute-start.14 = (bf16[96,768]{1,0:T(8,128)(2,1)}, bf16[96,768]{1,0:T(8,128)(2,1)}, u32[]{:S(2)}, u32[]{:S(2)}) collective-permute-start(bf16[96,768]{1,0:T(8,128)(2,1)} %get-tuple-element.600), channel_id=1, source_target_pairs={{0,1},{1,2},{2,3},{3,0},{4,5},{5,6},{6,7},{7,4},{8,9},{9,10},{10,1... | collective-permute-start | bytes 442376 | tf_op jit(solution)/shard_map/ppermute | solution.py:75
  11.1 54.2 %collective-permute-start.15 = (bf16[96,768]{1,0:T(8,128)(2,1)}, bf16[96,768]{1,0:T(8,128)(2,1)}, u32[]{:S(2)}, u32[]{:S(2)}) collective-permute-start(bf16[96,768]{1,0:T(8,128)(2,1)} %get-tuple-element.600), channel_id=1, source_target_pairs={{0,2},{1,3},{2,0},{3,1},{4,6},{5,7},{6,4},{7,5},{8,10},{9,11},{10,... | collective-permute-start | bytes 442376 | tf_op jit(solution)/shard_map/ppermute | solution.py:75
  12.1 58.0 %collective-permute-start.16 = (bf16[96,768]{1,0:T(8,128)(2,1)}, bf16[96,768]{1,0:T(8,128)(2,1)}, u32[]{:S(2)}, u32[]{:S(2)}) collective-permute-start(bf16[96,768]{1,0:T(8,128)(2,1)} %get-tuple-element.600), channel_id=1, source_target_pairs={{0,3},{1,0},{2,1},{3,2},{4,7},{5,4},{6,5},{7,6},{8,11},{9,8},{10,9... | collective-permute-start | bytes 442376 | tf_op jit(solution)/shard_map/ppermute | solution.py:75
  15.2 41.2 %collective-permute-start = (bf16[192,384]{1,0:T(8,128)(2,1)}, bf16[192,384]{1,0:T(8,128)(2,1)}, u32[]{:S(2)}, u32[]{:S(2)}) collective-permute-start(bf16[192,384]{1,0:T(8,128)(2,1)} %get-tuple-element.598), channel_id=1, source_target_pairs={{0,1},{1,2},{2,3},{3,0},{4,5},{5,6},{6,7},{7,4},{8,9},{9,10},{10,1... | collective-permute-start | bytes 442376 | tf_op jit(solution)/shard_map/ppermute | solution.py:75
  15.2 43.8 %collective-permute-start.1 = (bf16[192,384]{1,0:T(8,128)(2,1)}, bf16[192,384]{1,0:T(8,128)(2,1)}, u32[]{:S(2)}, u32[]{:S(2)}) collective-permute-start(bf16[192,384]{1,0:T(8,128)(2,1)} %get-tuple-element.598), channel_id=1, source_target_pairs={{0,2},{1,3},{2,0},{3,1},{4,6},{5,7},{6,4},{7,5},{8,10},{9,11},{10,... | collective-permute-start | bytes 442376 | tf_op jit(solution)/shard_map/ppermute | solution.py:75
  65.3 34.1 %collective-permute-start.3 = (bf16[768,384]{1,0:T(8,128)(2,1)}, bf16[768,384]{1,0:T(8,128)(2,1)S(1)}, u32[]{:S(2)}, u32[]{:S(2)}) collective-permute-start(bf16[768,384]{1,0:T(8,128)(2,1)} %bitcast.10), channel_id=1, source_target_pairs={{0,4},{4,0},{8,12},{12,8},{16,20},{20,16},{24,28},{28,24},{1,5},{5... | collective-permute-start | bytes 1769480 | tf_op jit(solution)/shard_map/ppermute | solution.py:70
  70.2 31.0 %collective-permute-start.4 = (bf16[768,384]{1,0:T(8,128)(2,1)}, bf16[768,384]{1,0:T(8,128)(2,1)S(1)}, u32[]{:S(2)}, u32[]{:S(2)}) collective-permute-start(bf16[768,384]{1,0:T(8,128)(2,1)} %bitcast.10), channel_id=1, source_target_pairs={{0,8},{4,12},{8,0},{12,4},{16,24},{20,28},{24,16},{28,20},{1,9},{5... | collective-permute-start | bytes 1769480 | tf_op jit(solution)/shard_map/ppermute | solution.py:70
  75.2 35.6 %collective-permute-start.19 = (bf16[768,384]{1,0:T(8,128)(2,1)S(1)}, bf16[768,384]{1,0:T(8,128)(2,1)}, u32[]{:S(2)}, u32[]{:S(2)}) collective-permute-start(bf16[768,384]{1,0:T(8,128)(2,1)S(1)} %bitcast.1028), channel_id=1, source_target_pairs={{0,8},{4,12},{8,0},{12,4},{16,24},{20,28},{24,16},{28,20},{1,9},{5... | collective-permute-start | bytes 1769480 | tf_op jit(solution)/shard_map/ppermute | solution.py:70
  76.5 36.7 %collective-permute-start.24 = (bf16[384,768]{1,0:T(8,128)(2,1)}, bf16[384,768]{1,0:T(8,128)(2,1)S(1)}, u32[]{:S(2)}, u32[]{:S(2)}) collective-permute-start(bf16[384,768]{1,0:T(8,128)(2,1)} %bitcast.32), channel_id=1, source_target_pairs={{0,16},{4,20},{8,24},{12,28},{16,0},{20,4},{24,8},{28,12},{1,17},{... | collective-permute-start | bytes 1769480 | tf_op jit(solution)/shard_map/ppermute | solution.py:70
  113.2 30.4 %collective-permute-start.27 = (bf16[384,384]{1,0:T(8,128)(2,1)S(1)}, bf16[384,384]{1,0:T(8,128)(2,1)S(1)}, u32[]{:S(2)}, u32[]{:S(2)}) collective-permute-start(bf16[384,384]{1,0:T(8,128)(2,1)S(1)} %slice.339), channel_id=1, source_target_pairs={{0,16},{4,20},{8,24},{12,28},{16,0},{20,4},{24,8},{28,12},{1,17},{... | collective-permute-start | bytes 884744 | tf_op jit(solution)/shard_map/ppermute | solution.py:70
  113.7 299.5 %collective-permute-start.18 = (bf16[384,768]{1,0:T(8,128)(2,1)}, bf16[384,768]{1,0:T(8,128)(2,1)}, u32[]{:S(2)}, u32[]{:S(2)}) collective-permute-start(bf16[384,768]{1,0:T(8,128)(2,1)} %bitcast.32), channel_id=1, source_target_pairs={{0,4},{4,0},{8,12},{12,8},{16,20},{20,16},{24,28},{28,24},{1,5},{5... | collective-permute-start | bytes 1769480 | tf_op jit(solution)/shard_map/ppermute | solution.py:70
  148.0 251.8 %collective-permute-start.17 = (bf16[768,384]{1,0:T(8,128)(2,1)S(1)}, bf16[768,384]{1,0:T(8,128)(2,1)}, u32[]{:S(2)}, u32[]{:S(2)}) collective-permute-start(bf16[768,384]{1,0:T(8,128)(2,1)S(1)} %bitcast.1030), channel_id=1, source_target_pairs={{0,4},{4,0},{8,12},{12,8},{16,20},{20,16},{24,28},{28,24},{1,5},{5... | collective-permute-start | bytes 1769480 | tf_op jit(solution)/shard_map/ppermute | solution.py:70
  153.8 280.7 %collective-permute-start.22 = (bf16[384,768]{1,0:T(8,128)(2,1)}, bf16[384,768]{1,0:T(8,128)(2,1)}, u32[]{:S(2)}, u32[]{:S(2)}) collective-permute-start(bf16[384,768]{1,0:T(8,128)(2,1)} %collective-permute-done.20), channel_id=1, source_target_pairs={{0,4},{4,0},{8,12},{12,8},{16,20},{20,16},{24,28},{28,24},{1,5},{5... | collective-permute-start | bytes 1769480 | tf_op jit(solution)/shard_map/ppermute | solution.py:70
  154.1 254.3 %collective-permute-start.21 = (bf16[768,384]{1,0:T(8,128)(2,1)}, bf16[768,384]{1,0:T(8,128)(2,1)}, u32[]{:S(2)}, u32[]{:S(2)}) collective-permute-start(bf16[768,384]{1,0:T(8,128)(2,1)} %collective-permute-done.19), channel_id=1, source_target_pairs={{0,4},{4,0},{8,12},{12,8},{16,20},{20,16},{24,28},{28,24},{1,5},{5... | collective-permute-start | bytes 1769480 | tf_op jit(solution)/shard_map/ppermute | solution.py:70
  155.0 225.8 %collective-permute-start.31 = (bf16[768,384]{1,0:T(8,128)(2,1)}, bf16[768,384]{1,0:T(8,128)(2,1)}, u32[]{:S(2)}, u32[]{:S(2)}) collective-permute-start(bf16[768,384]{1,0:T(8,128)(2,1)} %constant_dynamic-update-slice_fusion.2), channel_id=1, source_target_pairs={{0,4},{4,0},{8,12},{12,8},{16,20},{20,16},{24,28},{28,24},{1,5},{5... | collective-permute-start | bytes 1769480 | tf_op jit(solution)/shard_map/ppermute | solution.py:70
  380.8 59.1 %collective-permute-start.26 = (bf16[384,768]{1,0:T(8,128)(2,1)S(1)}, bf16[384,768]{1,0:T(8,128)(2,1)S(1)}, u32[]{:S(2)}, u32[]{:S(2)}) collective-permute-start(bf16[384,768]{1,0:T(8,128)(2,1)S(1)} %copy-done.80), channel_id=1, source_target_pairs={{0,4},{4,0},{8,12},{12,8},{16,20},{20,16},{24,28},{28,24},{1,5},{5... | collective-permute-start | bytes 1769480 | tf_op jit(solution)/shard_map/ppermute | solution.py:70
  684.3 75.9 %collective-permute-start.33 = (bf16[4,768,384]{2,1,0:T(8,128)(2,1)}, bf16[4,768,384]{2,1,0:T(8,128)(2,1)}, u32[]{:S(2)}, u32[]{:S(2)}) collective-permute-start(bf16[4,768,384]{2,1,0:T(8,128)(2,1)} %pad_maximum_fusion), channel_id=1, source_target_pairs={{0,4},{4,0},{8,12},{12,8},{16,20},{20,16},{24,28},{28,24},{1,5},{5... | collective-permute-start | bytes 7077896 | tf_op jit(solution)/shard_map/ppermute | solution.py:70
  702.3 64.3 %collective-permute-start.49 = (bf16[4,768,384]{2,1,0:T(8,128)(2,1)}, bf16[4,768,384]{2,1,0:T(8,128)(2,1)}, u32[]{:S(2)}, u32[]{:S(2)}) collective-permute-start(bf16[4,768,384]{2,1,0:T(8,128)(2,1)} %pad_maximum_fusion.1), channel_id=1, source_target_pairs={{0,4},{4,0},{8,12},{12,8},{16,20},{20,16},{24,28},{28,24},{1,5},{5... | collective-permute-start | bytes 7077896 | tf_op jit(solution)/shard_map/ppermute | solution.py:70
  713.0 57.3 %collective-permute-start.65 = (bf16[4,384,768]{2,1,0:T(8,128)(2,1)}, bf16[4,384,768]{2,1,0:T(8,128)(2,1)}, u32[]{:S(2)}, u32[]{:S(2)}) collective-permute-start(bf16[4,384,768]{2,1,0:T(8,128)(2,1)} %pad_maximum_fusion.2), channel_id=1, source_target_pairs={{0,4},{4,0},{8,12},{12,8},{16,20},{20,16},{24,28},{28,24},{1,5},{5... | collective-permute-start | bytes 7077896 | tf_op jit(solution)/shard_map/ppermute | solution.py:70
  779.4 31.3 %collective-permute-start.53 = (bf16[768,384]{1,0:T(8,128)(2,1)S(1)}, bf16[768,384]{1,0:T(8,128)(2,1)S(1)}, u32[]{:S(2)}, u32[]{:S(2)}) collective-permute-start(bf16[768,384]{1,0:T(8,128)(2,1)S(1)} %pad_maximum_fusion.16), channel_id=1, source_target_pairs={{0,16},{4,20},{8,24},{12,28},{16,0},{20,4},{24,8},{28,12},{1,17},{... | collective-permute-start | bytes 1769480 | tf_op jit(solution)/shard_map/ppermute | solution.py:70
  785.7 37.6 %collective-permute-start.69 = (bf16[384,768]{1,0:T(8,128)(2,1)S(1)}, bf16[384,768]{1,0:T(8,128)(2,1)S(1)}, u32[]{:S(2)}, u32[]{:S(2)}) collective-permute-start(bf16[384,768]{1,0:T(8,128)(2,1)S(1)} %pad_maximum_fusion.18), channel_id=1, source_target_pairs={{0,16},{4,20},{8,24},{12,28},{16,0},{20,4},{24,8},{28,12},{1,17},{... | collective-permute-start | bytes 1769480 | tf_op jit(solution)/shard_map/ppermute | solution.py:70
  798.0 30.6 %collective-permute-start.67 = (bf16[384,768]{1,0:T(8,128)(2,1)S(1)}, bf16[384,768]{1,0:T(8,128)(2,1)S(1)}, u32[]{:S(2)}, u32[]{:S(2)}) collective-permute-start(bf16[384,768]{1,0:T(8,128)(2,1)S(1)} %pad_maximum_fusion.17), channel_id=1, source_target_pairs={{0,8},{4,12},{8,0},{12,4},{16,24},{20,28},{24,16},{28,20},{1,9},{5... | collective-permute-start | bytes 1769480 | tf_op jit(solution)/shard_map/ppermute | solution.py:70
  799.9 30.2 %collective-permute-start.40 = (bf16[192,384]{1,0:T(8,128)(2,1)S(1)}, bf16[192,384]{1,0:T(8,128)(2,1)S(1)}, u32[]{:S(2)}, u32[]{:S(2)}) collective-permute-start(bf16[192,384]{1,0:T(8,128)(2,1)S(1)} %get-tuple-element.624), channel_id=1, source_target_pairs={{0,3},{1,0},{2,1},{3,2},{4,7},{5,4},{6,5},{7,6},{8,11},{9,8},{10,9... | collective-permute-start | bytes 442376 | tf_op jit(solution)/shard_map/ppermute | solution.py:75
  (377 other events, 2507.6 us)
Sparse Core Ops, SparseCore 0:
  673.0 46.3 all-reduce.6

commit v2 on v1

v2 whole, which is shorter than its diff:
```python
import jax
import jax.numpy as jnp
from jax import lax
from jax.experimental import pallas as pl
from jax.experimental.pallas import tpu as pltpu
from jax.sharding import PartitionSpec as P

D = 768
HEADS = 12
HEAD = 64
FEAT = 128
PAIRS = HEADS // 2
GROUP = 4 * HEAD
PIECES = 8
CHUNK = 4 * D // PIECES
QKV_BLOCKS = 3 * D // CHUNK
SLAB = (PAIRS + 1) * FEAT

norm_epsilon = 1e-05
low_type = jnp.bfloat16
wide_type = jnp.float32


def flip(value, bit):
    count = lax.axis_size("rep")
    return lax.ppermute(value, "rep", [(i, i ^ bit) for i in range(count)])


def spin(value, step):
    count = lax.axis_size("shard")
    return lax.ppermute(value, "shard", [(i, (i + step) % count) for i in range(count)])


def slide(value, step):
    count = lax.axis_size("shard")
    pairs = [(i, i + step) for i in range(count) if 0 <= i + step < count]
    return lax.ppermute(value, "shard", pairs)


def wide(value):
    return value.astype(wide_type)


def low(value):
    return value.astype(low_type)


def spread(own):
    half = own.shape[0] // 2
    from_x = flip(own, 2)
    from_y = flip(own, 4)
    diagonal = jnp.concatenate([flip(from_x[:half], 4), flip(from_y[half:], 2)], axis=0)
    even = [own, from_x, from_y, diagonal]
    return even, [flip(part, 1) for part in even]


def around(part):
    count, here = lax.axis_size("shard"), lax.axis_index("shard")
    full = jnp.zeros((count,) + part.shape, part.dtype)
    full = lax.dynamic_update_index_in_dim(full, part, here, 0)
    for step in range(1, count):
        full = lax.dynamic_update_index_in_dim(full, spin(part, step), (here - step) % count, 0)
    return full


def gather_pieces(part):
    full = around(part)
    return spread(full.reshape((-1,) + part.shape[1:]))


def scatter_shards(total):
    count, here = lax.axis_size("shard"), lax.axis_index("shard")
    blocks = total.reshape((count, total.shape[0] // count) + total.shape[1:])
    pick = lambda step: lax.dynamic_index_in_dim(blocks, (here + step) % count, 0, False)
    result = pick(0)
    for step in range(1, count):
        result = result + wide(spin(low(pick(step)), step))
    return result


def sum_pieces(even, odd):
    other = flip(odd, 1)
    half = even.shape[1] // 2
    both = lambda i, rows: wide(even[i, rows]) + wide(other[i, rows])
    upper, lower, every = slice(None, half), slice(half, None), slice(None)
    to_y = flip(low(both(3, upper)), 4)
    to_x = flip(low(both(3, lower)), 2)
    x_part = jnp.concatenate([both(1, upper) + wide(to_y), both(1, lower)], axis=0)
    y_part = jnp.concatenate([both(2, upper), both(2, lower) + wide(to_x)], axis=0)
    mine = both(0, every) + wide(flip(low(x_part), 2)) + wide(flip(low(y_part), 4))
    bit = PIECES
    while bit < lax.axis_size("rep"):
        mine = mine + wide(flip(low(mine), bit))
        bit *= 2
    return spread(low(scatter_shards(mine)))


def dot(a, b):
    return jnp.dot(a, b, preferred_element_type=wide_type)


def dot_nt(a, b):
    return lax.dot_general(a, b, (((1,), (1,)), ((), ())), preferred_element_type=wide_type)


def dot_tn(a, b):
    return lax.dot_general(a, b, (((0,), (0,)), ((), ())), preferred_element_type=wide_type)


def normalize(rows):
    centred = rows - jnp.mean(rows, axis=-1, keepdims=True)
    scale = lax.rsqrt(jnp.mean(centred * centred, axis=-1, keepdims=True) + norm_epsilon)
    return centred * scale, scale


def norm_backward(grad, normal, scale, gain):
    e = grad * gain
    return scale * (
        e
        - jnp.mean(e, axis=-1, keepdims=True)
        - normal * jnp.mean(e * normal, axis=-1, keepdims=True)
    )


def lane_index(shape):
    return lax.broadcasted_iota(jnp.int32, shape, len(shape) - 1)


def row_index(shape):
    return lax.broadcasted_iota(jnp.int32, shape, len(shape) - 2)


def left_half(shape):
    return lane_index(shape) < HEAD


def aligned(index, unit):
    return pl.multiple_of(index * unit, unit)


def with_ones(pair):
    left = left_half(pair.shape)
    one = jnp.ones_like(pair)
    return jnp.where(left, pair, one), jnp.where(left, one, pair)


def pack_state(even, odd, p):
    lane = lane_index(even.shape)
    packed = jnp.where(lane < HEAD, even, odd)
    sums = jnp.where(lane == HEAD + 2 * p, even, jnp.where(lane == 2 * p + 1, odd, 0.0))
    return packed, sums


def unpack_state(packed, sums, p):
    shape = packed.shape
    lane, row = lane_index(shape), row_index(shape)
    pick_even = low(jnp.where((row == HEAD + 2 * p) & (lane >= HEAD), 1.0, 0.0))
    pick_odd = low(jnp.where((row == 2 * p + 1) & (lane < HEAD), 1.0, 0.0))
    even = jnp.where(lane < HEAD, packed, dot(sums, pick_even))
    odd = jnp.where(lane < HEAD, dot(sums, pick_odd), packed)
    return low(even), low(odd)


def added(refs, b, rows):
    total = wide(refs[0][b, rows, :])
    for ref in refs[1:]:
        total = total + wide(ref[b, rows, :])
    return total


def states_at(refs, b, p):
    packed = added(refs, b, pl.ds(aligned(p, FEAT), FEAT))
    sums = low(added(refs, b, slice(PAIRS * FEAT, SLAB)))
    return unpack_state(packed, sums, p)


def qkv_kernel(place, tokens, vectors, maps, *refs):
    pieces = refs[:PIECES]
    normed, normed_t, mixed, w_out, fq, fk, fq_t, fk_t, state = refs[PIECES:]
    seqs = state.shape[0]
    length = tokens.shape[0] // seqs
    normal, _ = normalize(wide(tokens[...]))
    normed[...] = low(normal * vectors[0:1, :] + vectors[1:2, :])
    normed_t[...] = normed[...].T
    for k in range(PIECES):
        block = place[0] ^ k

        @pl.when(block < QKV_BLOCKS)
        def _():
            mixed[:, pl.ds(aligned(block, CHUNK), CHUNK)] = low(dot(normed[...], pieces[k][...]))

        @pl.when(block >= QKV_BLOCKS)
        def _():
            w_out[:, pl.ds(aligned(block - QKV_BLOCKS, CHUNK), CHUNK)] = pieces[k][...]

    for which, (f_t, f) in enumerate(((fq_t, fq), (fk_t, fk))):

        def group(g, carry):
            columns = mixed[:, pl.ds(aligned(which * (D // GROUP) + g, GROUP), GROUP)]
            u_t = dot_nt(maps[which * (D // GROUP) + g], columns)
            for a in range(4):
                u = u_t[a * HEAD : (a + 1) * HEAD]
                up = jnp.exp(u - jnp.max(u, axis=0, keepdims=True))
                down = jnp.exp(jnp.min(u, axis=0, keepdims=True) - u)
                feature = jnp.concatenate(
                    [
                        up / jnp.sum(up, axis=0, keepdims=True),
                        down / jnp.sum(down, axis=0, keepdims=True),
                    ],
                    axis=0,
                )
                feature = low(feature)
                rows = pl.ds(aligned(g * 4 + a, FEAT), FEAT)
                f_t[rows, :] = feature
                f[:, rows] = feature.T
            return carry

        lax.fori_loop(0, D // GROUP, group, 0)

    def pair(p, sums):
        result = []
        for b in range(seqs):
            here = slice(b * length, (b + 1) * length)
            v_even, v_odd = with_ones(mixed[here, pl.ds(aligned(2 * D // FEAT + p, FEAT), FEAT)])
            even = dot(fk_t[pl.ds(aligned(2 * p, FEAT), FEAT), here], v_even)
            odd = dot(fk_t[pl.ds(aligned(2 * p + 1, FEAT), FEAT), here], v_odd)
            packed, new = pack_state(even, odd, p)
            state[b, pl.ds(aligned(p, FEAT), FEAT), :] = low(packed)
            result.append(sums[b] + new)
        return tuple(result)

    sums = lax.fori_loop(
        0, PAIRS, pair, tuple(jnp.zeros((FEAT, FEAT), wide_type) for _ in range(seqs))
    )
    for b in range(seqs):
        state[b, PAIRS * FEAT :, :] = low(sums[b])


def attend_kernel(tokens, vectors, mixed, fq, fk_t, w_out, *refs):
    priors, (attended, inverse, resid, second, second_t) = refs[:-5], refs[-5:]
    seqs = priors[0].shape[0]
    length = tokens.shape[0] // seqs

    def pair(p, carry):
        for b in range(seqs):
            here = slice(b * length, (b + 1) * length)
            values = with_ones(mixed[here, pl.ds(aligned(2 * D // FEAT + p, FEAT), FEAT)])
            states = states_at(priors, b, p)
            found = []
            for side in range(2):
                rows = pl.ds(aligned(2 * p + side, FEAT), FEAT)
                scores = dot(fq[here, rows], fk_t[rows, here])
                scores = jnp.where(row_index(scores.shape) >= lane_index(scores.shape), scores, 0.0)
                found.append(dot(low(scores), values[side]) + dot(fq[here, rows], states[side]))
            left = left_half(found[0].shape)
            turned = [pltpu.roll(a, HEAD, 1) for a in found]
            over = 1.0 / jnp.where(left, turned[0], turned[1])
            columns = pl.ds(aligned(p, FEAT), FEAT)
            attended[here, columns] = low(jnp.where(left, found[0], found[1]) * over)
            inverse[here, columns] = over
        return carry

    lax.fori_loop(0, PAIRS, pair, 0)
    resid[...] = wide(tokens[...]) + dot(attended[...], w_out[...])
    normal, _ = normalize(resid[...])
    second[...] = low(normal * vectors[2:3, :] + vectors[3:4, :])
    second_t[...] = second[...].T


def mlp_kernel(second, second_t, cotangent, out_before, back_before, *refs):
    pieces = refs[:4]
    out_after, back_after, grads, up, down, ready = refs[4:]
    step = pl.program_id(0)
    block = pieces[0].shape[0]

    parts = grads_layout(second.shape[1], block)

    def copies(k, source):
        listed = []
        for i, (src, dst) in enumerate(parts):
            if dst[0] == "up":
                target = up.at[k, pl.ds(dst[1], dst[2]), :]
            else:
                target = down.at[k, pl.ds(dst[1], dst[2]), pl.ds(dst[3], CHUNK)]
            listed.append(
                pltpu.make_async_copy(source.at[pl.ds(src, dst[2]), :], target, ready.at[k, i])
            )
        return listed

    @pl.when(step == 0)
    def _():
        for k in range(4):
            for copy in copies(k, pieces[k]):
                copy.start()
        out_after[...] = out_before[...]
        back_after[...] = back_before[...]

    for copy in copies(step, pieces[0]):
        copy.wait()

    up_weight, down_weight = up[step], down[step]
    pre = dot(second[...], up_weight)
    inner = 0.7978845608 * (pre + 0.044715 * pre * pre * pre)
    bent = jnp.tanh(inner)
    hidden = low(0.5 * pre * (1.0 + bent))
    slope = 0.5 * (1.0 + bent) + 0.5 * pre * (1.0 - bent * bent) * (
        0.7978845608 * (1.0 + 3.0 * 0.044715 * pre * pre)
    )
    out_after[...] += dot(hidden, down_weight)
    d_pre = low(dot_nt(cotangent[...], down_weight) * slope)
    back_after[...] += dot_nt(d_pre, up_weight)
    d_up = low(dot(second_t[...], d_pre))
    d_down = low(dot_tn(hidden, cotangent[...]))
    for src, dst in parts:
        if dst[0] == "up":
            grads[0, src : src + dst[2], :] = d_up[dst[1] : dst[1] + dst[2]]
        else:
            grads[0, src : src + dst[2], :] = d_down[dst[1] : dst[1] + dst[2], dst[3] : dst[3] + CHUNK]


def grads_layout(width, block):
    shards = block // CHUNK
    up_rows = width // shards
    down_rows = CHUNK // shards
    parts = []
    for s in range(shards):
        base = s * (up_rows + 2 * down_rows)
        parts.append((base, ("up", s * up_rows, up_rows)))
        for side in range(2):
            parts.append(
                (
                    base + up_rows + side * down_rows,
                    ("down", s * down_rows, down_rows, side * CHUNK),
                )
            )
    return parts


def resid_kernel(out_sum, back_sum, resid, cotangent, vectors, w_out, attended, inverse, fq_t, *refs):
    block_out, d_resid, d_resid_low, d_vectors, d_num, d_den, state = refs
    seqs = state.shape[0]
    length = resid.shape[0] // seqs
    block_out[...] = low(out_sum[...])
    normal, scale = normalize(resid[...])
    grad = back_sum[...]
    d_vectors[0:1, :] = jnp.sum(grad * normal, axis=0, keepdims=True)
    d_vectors[1:2, :] = jnp.sum(grad, axis=0, keepdims=True)
    d_resid[...] = wide(cotangent[...]) + norm_backward(grad, normal, scale, vectors[2:3, :])
    d_resid_low[...] = low(d_resid[...])
    d_attended = dot_nt(d_resid_low[...], w_out[...])
    shape = (FEAT, FEAT)
    cross = low(
        jnp.where(left_half(shape) != (row_index(shape) < HEAD), -1.0 / HEAD, 0.0)
    )
    for p in range(PAIRS):
        columns = slice(p * FEAT, (p + 1) * FEAT)
        num = d_attended[:, columns] * inverse[:, columns]
        product = num * wide(attended[:, columns])
        top = low(product)
        rest = low(product - wide(top))
        d_num[:, columns] = low(num)
        d_den[:, columns] = low(dot(top, cross) + dot(rest, cross))

    def pair(p, sums):
        result = []
        for b in range(seqs):
            here = slice(b * length, (b + 1) * length)
            d_even, d_odd = joined(d_num, d_den, here, p)
            even = dot(fq_t[pl.ds(aligned(2 * p, FEAT), FEAT), here], d_even)
            odd = dot(fq_t[pl.ds(aligned(2 * p + 1, FEAT), FEAT), here], d_odd)
            packed, new = pack_state(even, odd, p)
            state[b, pl.ds(aligned(p, FEAT), FEAT), :] = low(packed)
            result.append(sums[b] + new)
        return tuple(result)

    sums = lax.fori_loop(
        0, PAIRS, pair, tuple(jnp.zeros((FEAT, FEAT), wide_type) for _ in range(seqs))
    )
    for b in range(seqs):
        state[b, PAIRS * FEAT :, :] = low(sums[b])


def joined(d_num, d_den, here, p):
    columns = pl.ds(aligned(p, FEAT), FEAT)
    num, den = d_num[here, columns], d_den[here, columns]
    left = left_half(num.shape)
    return jnp.where(left, num, den), jnp.where(left, den, num)


def softmax_backward(feature, grad):
    plus, minus = wide(feature[:HEAD]), wide(feature[HEAD:])
    d_plus, d_minus = grad[:HEAD], grad[HEAD:]
    d_plus = plus * (d_plus - jnp.sum(d_plus * plus, axis=0, keepdims=True))
    d_minus = minus * (d_minus - jnp.sum(d_minus * minus, axis=0, keepdims=True))
    return low(d_plus - d_minus)


def local_kernel(mixed, fq_t, fk, fk_t, d_num, d_den, *refs):
    priors, (d_uq_t, d_fk_t, d_values) = refs[:-3], refs[-3:]
    seqs = priors[0].shape[0]
    length = mixed.shape[0] // seqs

    def pair(p, carry):
        for b in range(seqs):
            here = slice(b * length, (b + 1) * length)
            values = with_ones(mixed[here, pl.ds(aligned(2 * D // FEAT + p, FEAT), FEAT)])
            outer = joined(d_num, d_den, here, p)
            states = states_at(priors, b, p)
            found = []
            for side in range(2):
                rows = pl.ds(aligned(2 * p + side, FEAT), FEAT)
                q_t, k_t = fq_t[rows, here], fk_t[rows, here]
                link = dot_nt(outer[side], values[side])
                row, lane = row_index(link.shape), lane_index(link.shape)
                link = low(jnp.where(row >= lane, link, 0.0))
                d_q = dot_nt(k_t, link) + dot_nt(states[side], outer[side])
                d_uq_t[pl.ds(aligned(2 * p + side, HEAD), HEAD), here] = softmax_backward(q_t, d_q)
                d_fk_t[rows, here] = dot(q_t, link)
                scores = dot(fk[here, rows], q_t)
                scores = low(jnp.where(row <= lane, scores, 0.0))
                found.append(dot(scores, outer[side]))
            left = left_half(found[0].shape)
            d_values[here, pl.ds(aligned(p, FEAT), FEAT)] = jnp.where(left, found[0], found[1])
        return carry

    lax.fori_loop(0, PAIRS, pair, 0)


def mixed_kernel(mixed, fk, fk_t, maps, d_uq_t, d_fk_t, d_values, *refs):
    laters, (d_mixed, d_maps, d_uk_t) = refs[:-3], refs[-3:]
    seqs = laters[0].shape[0]
    length = mixed.shape[0] // seqs

    def pair(p, carry):
        for b in range(seqs):
            here = slice(b * length, (b + 1) * length)
            values = with_ones(mixed[here, pl.ds(aligned(2 * D // FEAT + p, FEAT), FEAT)])
            states = states_at(laters, b, p)
            found = []
            for side in range(2):
                rows = pl.ds(aligned(2 * p + side, FEAT), FEAT)
                d_k = d_fk_t[rows, here] + dot_nt(states[side], values[side])
                d_uk_t[pl.ds(aligned(2 * p + side, HEAD), HEAD), here] = softmax_backward(
                    fk_t[rows, here], d_k
                )
                found.append(dot(fk[here, rows], states[side]))
            left = left_half(found[0].shape)
            total = d_values[here, pl.ds(aligned(p, FEAT), FEAT)] + jnp.where(
                left, found[0], found[1]
            )
            d_mixed[here, pl.ds(aligned(2 * D // FEAT + p, FEAT), FEAT)] = low(total)
        return carry

    lax.fori_loop(0, PAIRS, pair, 0)
    for which, d_u_t in enumerate((d_uq_t, d_uk_t)):

        def group(g, carry):
            index = which * (D // GROUP) + g
            d_u = d_u_t[pl.ds(aligned(g, GROUP), GROUP), :]
            columns = pl.ds(aligned(index, GROUP), GROUP)
            d_maps[index] = low(dot(d_u, mixed[:, columns]))
            d_mixed[:, columns] = low(dot(d_u.T, maps[index]))
            return carry

        lax.fori_loop(0, D // GROUP, group, 0)


def in_grads_kernel(place, normed_t, d_mixed, attended, d_resid_low, grads, *, first):
    for i in range(PIECES // 2):
        block = place[0] ^ (2 * i + first)

        @pl.when(block < QKV_BLOCKS)
        def _():
            columns = pl.ds(aligned(block, CHUNK), CHUNK)
            grads[i] = low(dot(normed_t[...], d_mixed[:, columns]))

        @pl.when(block >= QKV_BLOCKS)
        def _():
            columns = pl.ds(aligned(block - QKV_BLOCKS, CHUNK), CHUNK)
            grads[i] = low(dot_tn(attended[...], d_resid_low[:, columns]))


def input_kernel(place, tokens, vectors, d_mixed, d_resid, *refs):
    pieces = refs[:PIECES]
    grad_tokens, d_vectors, total = refs[PIECES:]
    total[...] = jnp.zeros_like(total)
    for k in range(PIECES):
        block = place[0] ^ k

        @pl.when(block < QKV_BLOCKS)
        def _():
            columns = pl.ds(aligned(block, CHUNK), CHUNK)
            total[...] += dot_nt(d_mixed[:, columns], pieces[k][...])

    normal, scale = normalize(wide(tokens[...]))
    grad = total[...]
    d_vectors[0:1, :] = jnp.sum(grad * normal, axis=0, keepdims=True)
    d_vectors[1:2, :] = jnp.sum(grad, axis=0, keepdims=True)
    grad_tokens[...] = low(d_resid[...] + norm_backward(grad, normal, scale, vectors[0:1, :]))


def lay_in_kernel(place, *refs):
    pieces, (qkv, out) = refs[:PIECES], refs[PIECES:]
    for k in range(PIECES):
        block = place[0] ^ k

        @pl.when(block < QKV_BLOCKS)
        def _():
            qkv[:, pl.ds(aligned(block, CHUNK), CHUNK)] = wide(pieces[k][...])

        @pl.when(block >= QKV_BLOCKS)
        def _():
            out[:, pl.ds(aligned(block - QKV_BLOCKS, CHUNK), CHUNK)] = wide(pieces[k][...])


def lay_mlp_kernel(place, *refs):
    pieces, (up, down) = refs[:PIECES], refs[PIECES:]
    up_rows, down_rows = up.shape[1], down.shape[1]
    for k in range(PIECES):
        block = place[0] ^ k
        up[block] = pieces[k][:up_rows, :]
        for side in range(2):
            start = up_rows + side * down_rows
            down[block, :, side * CHUNK : (side + 1) * CHUNK] = wide(
                pieces[k][start : start + down_rows, :]
            )


def whole(shape, dtype=low_type):
    return jax.ShapeDtypeStruct(shape, dtype)


def scalar_first(count):
    return [pl.BlockSpec(memory_space=pltpu.SMEM)] + [
        pl.BlockSpec(memory_space=pltpu.VMEM) for _ in range(count)
    ]


def interleave(even, odd):
    return [part for both in zip(even, odd) for part in both]


def shards(
    tokens,
    gain_attn,
    bias_attn,
    w_qkv,
    w_feature,
    w_out,
    gain_mlp,
    bias_mlp,
    w_up,
    w_down,
    cotangent,
):
    shard_count = lax.axis_size("shard")
    place = lax.axis_index("rep") % PIECES
    spot = place.reshape(1).astype(jnp.int32)
    seqs, length, _ = tokens.shape
    count = seqs * length
    rows = w_qkv.shape[0]
    fine = CHUNK // shard_count

    small = jnp.concatenate(
        [w_feature.reshape(-1), gain_attn, bias_attn, gain_mlp, bias_mlp]
    ).reshape(-1, rows)
    small = around(small)
    feature_weight = small[:, :FEAT].reshape(shard_count, rows, FEAT).reshape(D, FEAT)
    vectors = wide(small[:, FEAT:].transpose(1, 0, 2).reshape(4, D))
    blocks = feature_weight.reshape(D // GROUP, 4, HEAD, 2, HEAD)
    maps = (
        jnp.einsum("gaiwo,ab->wgaobi", blocks, jnp.eye(4, dtype=low_type))
        .reshape(2 * D // GROUP, GROUP, GROUP)
        .astype(low_type)
    )

    part_in = lax.dynamic_slice_in_dim(
        jnp.concatenate([w_qkv, w_out], axis=1), place * CHUNK, CHUNK, 1
    )
    in_even, in_odd = gather_pieces(part_in)
    in_pieces = interleave(in_even, in_odd)
    part_up = lax.dynamic_index_in_dim(
        w_up.reshape(rows, shard_count, PIECES, fine), place, 2, False
    ).reshape(rows, CHUNK)
    part_down = lax.dynamic_slice_in_dim(w_down, place * fine, fine, 0)
    mlp_even, mlp_odd = gather_pieces(
        jnp.concatenate([part_up, part_down[:, :CHUNK], part_down[:, CHUNK:]], axis=0)
    )

    flat = tokens.reshape(count, D)
    flat_cotangent = cotangent.reshape(count, D)
    normed, normed_t, mixed, out_weight, fq, fk, fq_t, fk_t, key_state = pl.pallas_call(
        qkv_kernel,
        out_shape=(
            whole((count, D)),
            whole((D, count)),
            whole((count, 3 * D)),
            whole((D, D)),
            whole((count, HEADS * FEAT)),
            whole((count, HEADS * FEAT)),
            whole((HEADS * FEAT, count)),
            whole((HEADS * FEAT, count)),
            whole((seqs, SLAB, FEAT)),
        ),
        in_specs=scalar_first(3 + PIECES),
        name="qkv",
    )(spot, flat, vectors, maps, *in_pieces)
    priors = [slide(key_state, step) for step in range(1, shard_count)]
    attended, inverse, resid, second, second_t = pl.pallas_call(
        attend_kernel,
        out_shape=(
            whole((count, D)),
            whole((count, D), wide_type),
            whole((count, D), wide_type),
            whole((count, D)),
            whole((D, count)),
        ),
        name="attend",
    )(flat, vectors, mixed, fq, fk_t, out_weight, *priors)

    def mlp(out_before, back_before, pieces, name):
        block = pieces[0].shape[0]
        fixed = lambda shape: pl.BlockSpec(shape, lambda i: (0, 0))
        return pl.pallas_call(
            mlp_kernel,
            grid=(4,),
            in_specs=[
                fixed((count, D)),
                fixed((D, count)),
                fixed((count, D)),
                fixed((count, D)),
                fixed((count, D)),
            ]
            + [pl.BlockSpec(memory_space=pl.ANY)] * 4,
            out_specs=(
                fixed((count, D)),
                fixed((count, D)),
                pl.BlockSpec((1, block, CHUNK), lambda i: (i, 0, 0)),
            ),
            out_shape=(
                whole((count, D), wide_type),
                whole((count, D), wide_type),
                whole((4, block, CHUNK)),
            ),
            scratch_shapes=[
                pltpu.VMEM((4, D, CHUNK), low_type),
                pltpu.VMEM((4, CHUNK, D), low_type),
                pltpu.SemaphoreType.DMA((4, 3 * shard_count)),
            ],
            name=name,
        )(second, second_t, flat_cotangent, out_before, back_before, *pieces)

    out_sum, back_sum, mlp_grads_odd = mlp(resid, jnp.zeros_like(resid), mlp_odd, "mlp_odd")
    out_sum, back_sum, mlp_grads_even = mlp(out_sum, back_sum, mlp_even, "mlp_even")
    block_out, d_resid, d_resid_low, d_vectors_two, d_num, d_den, query_state = pl.pallas_call(
        resid_kernel,
        out_shape=(
            whole((count, D)),
            whole((count, D), wide_type),
            whole((count, D)),
            whole((2, D), wide_type),
            whole((count, D)),
            whole((count, D)),
            whole((seqs, SLAB, FEAT)),
        ),
        name="resid",
    )(out_sum, back_sum, resid, flat_cotangent, vectors, out_weight, attended, inverse, fq_t)
    laters = [slide(query_state, -step) for step in range(1, shard_count)]
    d_uq_t, d_fk_t, d_values = pl.pallas_call(
        local_kernel,
        out_shape=(
            whole((D, count)),
            whole((HEADS * FEAT, count), wide_type),
            whole((count, D), wide_type),
        ),
        name="local",
    )(mixed, fq_t, fk, fk_t, d_num, d_den, *priors)
    d_mixed, d_maps, _ = pl.pallas_call(
        mixed_kernel,
        out_shape=(
            whole((count, 3 * D)),
            whole((2 * D // GROUP, GROUP, GROUP)),
            whole((D, count)),
        ),
        name="mixed",
    )(mixed, fk, fk_t, maps, d_uq_t, d_fk_t, d_values, *laters)

    def in_grads(first):
        return pl.pallas_call(
            lambda *refs: in_grads_kernel(*refs, first=first),
            out_shape=whole((PIECES // 2, D, CHUNK)),
            in_specs=scalar_first(4),
            name="in_grads",
        )(spot, normed_t, d_mixed, attended, d_resid_low)

    in_grads_odd = in_grads(1)
    in_grads_even = in_grads(0)
    grad_tokens, d_vectors_one = pl.pallas_call(
        input_kernel,
        out_shape=(whole((count, D)), whole((2, D), wide_type)),
        in_specs=scalar_first(4 + PIECES),
        scratch_shapes=[pltpu.VMEM((count, D), wide_type)],
        name="input",
    )(spot, flat, vectors, d_mixed, d_resid, *in_pieces)

    mlp_sums = interleave(*sum_pieces(mlp_grads_even, mlp_grads_odd))
    in_sums = interleave(*sum_pieces(in_grads_even, in_grads_odd))
    grad_qkv, grad_out = pl.pallas_call(
        lay_in_kernel,
        out_shape=(whole((rows, 3 * D), wide_type), whole((rows, D), wide_type)),
        in_specs=scalar_first(PIECES),
        name="lay_in",
    )(spot, *in_sums)
    grad_up, grad_down = pl.pallas_call(
        lay_mlp_kernel,
        out_shape=(whole((PIECES, rows, CHUNK)), whole((PIECES, fine, D), wide_type)),
        in_specs=scalar_first(PIECES),
        name="lay_mlp",
    )(spot, *mlp_sums)
    grad_up = (
        wide(grad_up)
        .reshape(PIECES, rows, shard_count, fine)
        .transpose(1, 2, 0, 3)
        .reshape(rows, -1)
    )
    grad_down = grad_down.reshape(-1, D)

    d_maps = d_maps.reshape(2, D // GROUP, 4, HEAD, 4, HEAD)
    d_maps = jnp.stack([d_maps[:, :, a, :, a, :] for a in range(4)], axis=2)
    d_maps = d_maps.transpose(1, 2, 4, 0, 3).reshape(shard_count, -1)
    d_vectors = jnp.concatenate([d_vectors_one, d_vectors_two], axis=0)
    d_vectors = d_vectors.reshape(4, shard_count, rows).transpose(1, 0, 2)
    tiny = jnp.concatenate([wide(d_maps), d_vectors.reshape(shard_count, -1)], axis=1)
    tiny = tiny.reshape(-1, rows)
    bit = 1
    while bit < lax.axis_size("rep"):
        tiny = tiny + wide(flip(low(tiny), bit))
        bit *= 2
    tiny = scatter_shards(tiny)
    grad_feature = tiny[:FEAT].reshape(rows, FEAT)
    return (
        block_out.reshape(tokens.shape),
        grad_tokens.reshape(tokens.shape),
        tiny[FEAT],
        tiny[FEAT + 1],
        grad_qkv,
        grad_feature,
        grad_out,
        tiny[FEAT + 2],
        tiny[FEAT + 3],
        grad_up,
        grad_down,
    )


def solution(mesh):
    placed = (
        P("rep", "shard", None),
        P("shard"),
        P("shard"),
        P("shard", None),
        P("shard", None),
        P("shard", None),
        P("shard"),
        P("shard"),
        P("shard", None),
        P("shard", None),
        P("rep", "shard", None),
    )
    return jax.shard_map(
        shards,
        mesh=mesh,
        in_specs=placed,
        out_specs=(
            P("rep", "shard", None),
            P("rep", "shard", None),
            P("shard"),
            P("shard"),
            P("shard", None),
            P("shard", None),
            P("shard", None),
            P("shard"),
            P("shard"),
            P("shard", None),
            P("shard", None),
        ),
        check_vma=False,
    )
```

time: 919 us -> 470 us (0.51)
  matrix products: 221 us -> 0 us
  local copies, waits for them, and re-layouts: 206 us -> 48.1 us
  blocking collectives: 152 us -> 0 us
  Pallas kernels: 0 us -> 126 us
  waiting for transfers between devices: 89.1 us -> 161 us
  other arithmetic: 93.5 us -> 22.9 us
  starting transfers between devices: 121 us -> 101 us
  between operations: 19 us -> 2.04 us
    dot_general x150 -> x0, matrix products: 198 us -> none  [the longest x16 19.4 us: shards(): jnp.dot(hidden_low.T, grad_out, preferred_element_type=jnp.float32)]
    all_gather x9 -> x0, blocking collectives: 129 us -> none  [the longest x4 53.1 us: prefix(): lax.all_gather(part.astype(kind), axis)]
    pallas_call x0 -> x12, Pallas kernels: none -> 126 us  [the longest x2 32.1 us: mlp(): pl.pallas_call(mlp_kernel, grid=(4,), in_specs=[fixed((count, D)), fixed(...]
    ppermute x63 -> x45, starting transfers between devices: 86.5 us -> 39.8 us  [flip(): return lax.ppermute(value, 'rep', [(i, i ^ bit) for i in range(count)])]
    ppermute x18, waiting for transfers between devices: 14.3 us -> 55.4 us  [spin(): lax.ppermute(value, 'shard', [(i, (i + step) % count) for i in range(coun...]
    concatenate x17 -> x0, local copies, waits for them, and re-layouts: 34.7 us -> none  [the longest x16 33.1 us: featurize(): jnp.concatenate([jax.nn.softmax(inputs, axis=-1), jax.nn.softmax(-inputs,...]
    ppermute x0 -> x6, waiting for transfers between devices: none -> 34.6 us  [slide(): return lax.ppermute(value, 'shard', pairs)]
    unnamed x635 -> x88, local copies, waits for them, and re-layouts: 41 us -> 6.77 us
  transfers between devices with their start and end apart: 82 -> 69, of which waited for: 18 -> 21; matrix products, arithmetic and copies ran while one was open for 35% -> 11% of each run, Pallas kernels for 0% -> 23%
where the time goes in v2:
time: 470 us; the launch traced here: 461 us
  waiting for transfers between devices  161 us (34%)
  Pallas kernels  126 us (27%)
  starting transfers between devices  101 us (21%)
  local copies, waits for them, and re-layouts  48.1 us (10%)
  other arithmetic  22.9 us (5%)
    ppermute x45, waiting for transfers between devices, flip(): return lax.ppermute(value, 'rep', [(i, i ^ bit) for i in range(count)])  71 us
    ppermute x18, waiting for transfers between devices, spin(): lax.ppermute(value, 'shard', [(i, (i + step) % count) for i in range(coun...  55.4 us
    ppermute x45, starting transfers between devices, flip(): return lax.ppermute(value, 'rep', [(i, i ^ bit) for i in range(count)])  39.8 us
    ppermute x6, waiting for transfers between devices, slide(): return lax.ppermute(value, 'shard', pairs)  34.6 us
    ppermute x18, starting transfers between devices, spin(): lax.ppermute(value, 'shard', [(i, (i + step) % count) for i in range(coun...  34.5 us
    pallas_call x2, Pallas kernels, mlp(): pl.pallas_call(mlp_kernel, grid=(4,), in_specs=[fixed((count, D)), fixed(...  32.1 us
    ppermute x6, starting transfers between devices, slide(): return lax.ppermute(value, 'shard', pairs)  26.8 us
    pallas_call x1, Pallas kernels, shards(): pl.pallas_call(qkv_kernel, out_shape=(whole((count, D)), whole((D, count)...  16.6 us
  transfers between devices with their start and end apart: 69, of which 21 were waited for; matrix products, arithmetic and copies ran while one was open for 11% of the time, Pallas kernels for 23%

profile of v2, /device:TPU:9, one launch (start us, length us, event | category | flops | bytes accessed | tf_op | source)
XLA Modules:
  0.0 461.1 jit_solution(13051048436056150349)
XLA Ops:
  13.4 29.0 %collective-permute-done.4 = bf16[192,384]{1,0:T(8,128)(2,1)} collective-permute-done((bf16[192,384]{1,0:T(8,128)(2,1)S(1)}, bf16[192,384]{1,0:T(8,128)(2,1)}, u32[]{:S(2)}, u32[]{:S(2)}) %collective-permute-start.4) | collective-permute-done | bytes 147488 | tf_op jit(solution)/shard_map/ppermute | solution.py:31
  49.9 10.3 %collective-permute-done.7.refs_2_ = bf16[768,384]{1,0:T(8,128)(2,1)} collective-permute-done((bf16[768,384]{1,0:T(8,128)(2,1)S(1)}, bf16[768,384]{1,0:T(8,128)(2,1)}, u32[]{:S(2)}, u32[]{:S(2)}) %collective-permute-start.7) | collective-permute-done | bytes 589856 | tf_op jit(solution)/shard_map/ppermute | solution.py:26
  62.5 24.1 %collective-permute-done.9.refs_4_ = bf16[768,384]{1,0:T(8,128)(2,1)} collective-permute-done((bf16[768,384]{1,0:T(8,128)(2,1)S(1)}, bf16[768,384]{1,0:T(8,128)(2,1)}, u32[]{:S(2)}, u32[]{:S(2)}) %collective-permute-start.9) | collective-permute-done | bytes 589856 | tf_op jit(solution)/shard_map/ppermute | solution.py:26
  93.5 6.3 %collective-permute-done.12 = bf16[384,384]{1,0:T(8,128)(2,1)S(1)} collective-permute-done((bf16[384,384]{1,0:T(8,128)(2,1)S(1)}, bf16[384,384]{1,0:T(8,128)(2,1)S(1)}, u32[]{:S(2)}, u32[]{:S(2)}) %collective-permute-start.12) | collective-permute-done | bytes 294944 | tf_op jit(solution)/shard_map/ppermute | solution.py:26
  118.5 16.6 %qkv.1 = (bf16[512,768]{1,0:T(8,128)(2,1)}, bf16[768,512]{1,0:T(8,128)(2,1)}, bf16[512,2304]{1,0:T(8,128)(2,1)}, bf16[768,768]{1,0:T(8,128)(2,1)}, bf16[512,1536...) custom-call(s32[1]{0:T(128)} %bitcast.6.place.refs_0_, ...), custom_call_target="tpu_custom_call" | custom-call | tf_op jit(solution)/shard_map/qkv/pallas_call | solution.py:592
  139.7 9.8 %collective-permute-done.14.refs_0_ = bf16[2,896,128]{2,1,0:T(8,128)(2,1)S(1)} collective-permute-done((bf16[2,896,128]{2,1,0:T(8,128)(2,1)}, bf16[2,896,128]{2,1,0:T(8,128)(2,1)S(1)}, u32[]{:S(2)}, u32[]{:S(2)}) %collective-permute-start.14) | collective-permute-done | bytes 458784 | tf_op jit(solution)/shard_map/ppermute | solution.py:37
  153.8 19.1 %collective-permute-done.15.refs_1_ = bf16[2,896,128]{2,1,0:T(8,128)(2,1)S(1)} collective-permute-done((bf16[2,896,128]{2,1,0:T(8,128)(2,1)S(1)}, bf16[2,896,128]{2,1,0:T(8,128)(2,1)S(1)}, u32[]{:S(2)}, u32[]{:S(2)}) %collective-permute-start.15) | collective-permute-done | bytes 458784 | tf_op jit(solution)/shard_map/ppermute | solution.py:37
  174.4 10.8 %attend.1 = (bf16[512,768]{1,0:T(8,128)(2,1)}, f32[512,768]{1,0:T(8,128)}, f32[512,768]{1,0:T(8,128)}, bf16[512,768]{1,0:T(8,128)(2,1)}, bf16[768,512]{1,0:T(8,128)(2,1)}) custom-call(bf16[512,768]{1,0:T(8,128)(2,1)} %bitcast.143, f32[4,768]{1,0:T(4,128)} %reshape.186.vectors, bf16[512,2304]{1,0:T(8,128)(2,1)} %get-tuple-element.48.mixed, ...), custom_call_target="tpu_custom_call" | custom-call | tf_op jit(solution)/shard_map/attend/pallas_call | solution.py:609
  186.4 16.1 %mlp_odd.1 = (f32[512,768]{1,0:T(8,128)}, f32[512,768]{1,0:T(8,128)}, bf16[4,1536,384]{2,1,0:T(8,128)(2,1)}) custom-call(bf16[512,768]{1,0:T(8,128)(2,1)} %get-tuple-element.53.second, bf16[768,512]{1,0:T(8,128)(2,1)} %get-tuple-element.54.second_t, bf16[512,768]{1,0:T(8,128)(2,1)} %bitcast.139, f32[512,768]{1,0:T(8,128)} %get-tuple-element.55.out_before.resid, ...), custom_call_target="tpu_custom_call" | custom-call | tf_op jit(solution)/shard_map/mlp_odd/pallas_call | solution.py:624
  203.0 16.1 %mlp_even.1 = (f32[512,768]{1,0:T(8,128)}, f32[512,768]{1,0:T(8,128)}, bf16[4,1536,384]{2,1,0:T(8,128)(2,1)}) custom-call(bf16[512,768]{1,0:T(8,128)(2,1)} %get-tuple-element.53.second, bf16[768,512]{1,0:T(8,128)(2,1)} %get-tuple-element.54.second_t, bf16[512,768]{1,0:T(8,128)(2,1)} %bitcast.140, f32[512,768]{1,0:T(8,128)} %get-tuple-element.56.out_before, ...), custom_call_target="tpu_custom_call" | custom-call | tf_op jit(solution)/shard_map/mlp_even/pallas_call | solution.py:624
  219.1 10.0 %resid.1 = (bf16[512,768]{1,0:T(8,128)(2,1)}, f32[512,768]{1,0:T(8,128)}, bf16[512,768]{1,0:T(8,128)(2,1)}, f32[2,768]{1,0:T(2,128)}, bf16[512,768]{1,0:T(8,128)...) custom-call(f32[512,768]{1,0:T(8,128)} %get-tuple-element.58.out_sum, ...), custom_call_target="tpu_custom_call" | custom-call | tf_op jit(solution)/shard_map/resid/pallas_call | solution.py:655
  229.1 16.9 %collective-permute-start.28 = (bf16[2,896,128]{2,1,0:T(8,128)(2,1)}, bf16[2,896,128]{2,1,0:T(8,128)(2,1)S(1)}, u32[]{:S(2)}, u32[]{:S(2)}) collective-permute-start(bf16[2,896,128]{2,1,0:T(8,128)(2,1)} %get-tuple-element.70), channel_id=1, source_target_pairs={{1,0},{2,1},{3,2},{5,4},{6,5},{7,6},{9,8},{10,9},{11,10},{13,12},{... | collective-permute-start | bytes 1376264 | tf_op jit(solution)/shard_map/ppermute | solution.py:37
  248.2 15.4 %local.1 = (bf16[768,512]{1,0:T(8,128)(2,1)}, f32[1536,512]{1,0:T(8,128)}, f32[512,768]{1,0:T(8,128)}) custom-call(bf16[512,2304]{1,0:T(8,128)(2,1)} %get-tuple-element.48.mixed, bf16[1536,512]{1,0:T(8,128)(2,1)} %get-tuple-element.62.fq_t, bf16[512,1536]{1,0:T(8,128)(2,1)} %get-tuple-element.64.fk, bf16[1536,512]{1,0:T(8,128)(2,1)} %get-tuple-element.50.fk_t, ...), custom_call_target="tpu_custom_call" | custom-call | tf_op jit(solution)/shard_map/local/pallas_call | solution.py:669
  270.2 12.2 %mixed.1 = (bf16[512,2304]{1,0:T(8,128)(2,1)}, bf16[6,256,256]{2,1,0:T(8,128)(2,1)}, bf16[768,512]{1,0:T(8,128)(2,1)}) custom-call(bf16[512,2304]{1,0:T(8,128)(2,1)} %get-tuple-element.48.mixed, bf16[512,1536]{1,0:T(8,128)(2,1)} %get-tuple-element.64.fk, bf16[1536,512]{1,0:T(8,128)(2,1)} %get-tuple-element.50.fk_t, bf16[6,256,256]{2,1,0:T(8,128)(2,1)} %reshape.166.maps, ...), custom_call_target="tpu_custom_call" | custom-call | tf_op jit(solution)/shard_map/mixed/pallas_call | solution.py:678
  282.4 6.1 %in_grads.3 = bf16[4,768,384]{2,1,0:T(8,128)(2,1)} custom-call(s32[1]{0:T(128)} %bitcast.6.place.refs_0_, bf16[768,512]{1,0:T(8,128)(2,1)} %get-tuple-element.77.refs_1_, bf16[512,2304]{1,0:T(8,128)(2,1)} %get-tuple-element.71.d_mixed.refs_2_, bf16[512,768]{1,0:T(8,128)(2,1)} %get-tuple-element.60.attended.refs_3_, bf16[512,768]{1,0:T(8,128)(2,1)} %get-tuple-element.78.refs_4_), custom_call_target="tpu_custom_call" | custom-call | tf_op jit(solution)/shard_map/in_grads/pallas_call | solution.py:689
  289.4 6.1 %in_grads.2 = bf16[4,768,384]{2,1,0:T(8,128)(2,1)} custom-call(s32[1]{0:T(128)} %bitcast.6.place.refs_0_, bf16[768,512]{1,0:T(8,128)(2,1)} %get-tuple-element.77.refs_1_, bf16[512,2304]{1,0:T(8,128)(2,1)} %get-tuple-element.71.d_mixed.refs_2_, bf16[512,768]{1,0:T(8,128)(2,1)} %get-tuple-element.60.attended.refs_3_, bf16[512,768]{1,0:T(8,128)(2,1)} %get-tuple-element.78.refs_4_), custom_call_target="tpu_custom_call" | custom-call | tf_op jit(solution)/shard_map/in_grads/pallas_call | solution.py:689
  299.1 9.8 %input.1 = (bf16[512,768]{1,0:T(8,128)(2,1)}, f32[2,768]{1,0:T(2,128)}) custom-call(s32[1]{0:T(128)} %bitcast.6.place.refs_0_, bf16[512,768]{1,0:T(8,128)(2,1)} %bitcast.144, f32[4,768]{1,0:T(4,128)} %reshape.186.vectors, bf16[512,2304]{1,0:T(8,128)(2,1)} %get-tuple-element.71.d_mixed.refs_2_, f32[512,768]{1,0:T(8,128)} %get-tuple-element.72.d_resid, ...), custom_call_target="tpu_custom_call" | custom-call | tf_op jit(solution)/shard_map/input/pallas_call | solution.py:698
  324.9 8.0 %collective-permute-done.54 = bf16[768,384]{1,0:T(8,128)(2,1)} collective-permute-done((bf16[768,384]{1,0:T(8,128)(2,1)}, bf16[768,384]{1,0:T(8,128)(2,1)}, u32[]{:S(2)}, u32[]{:S(2)}) %collective-permute-start.54) | collective-permute-done | bytes 589856 | tf_op jit(solution)/shard_map/ppermute | solution.py:26
  347.4 13.0 %collective-permute-start.43 = (bf16[192,384]{1,0:T(8,128)(2,1)S(1)}, bf16[192,384]{1,0:T(8,128)(2,1)S(1)}, u32[]{:S(2)}, u32[]{:S(2)}) collective-permute-start(bf16[192,384]{1,0:T(8,128)(2,1)S(1)} %get-tuple-element.108), channel_id=1, source_target_pairs={{0,2},{1,3},{2,0},{3,1},{4,6},{5,7},{6,4},{7,5},{8,10},{9,11},{10,... | collective-permute-start | bytes 442376 | tf_op jit(solution)/shard_map/ppermute | solution.py:31
  360.3 10.4 %collective-permute-done.55 = bf16[1536,384]{1,0:T(8,128)(2,1)} collective-permute-done((bf16[1536,384]{1,0:T(8,128)(2,1)}, bf16[1536,384]{1,0:T(8,128)(2,1)}, u32[]{:S(2)}, u32[]{:S(2)}) %collective-permute-start.55) | collective-permute-done | bytes 1179680 | tf_op jit(solution)/shard_map/ppermute | solution.py:26
  370.7 10.9 %collective-permute-start.44 = (bf16[192,384]{1,0:T(8,128)(2,1)S(1)}, bf16[192,384]{1,0:T(8,128)(2,1)S(1)}, u32[]{:S(2)}, u32[]{:S(2)}) collective-permute-start(bf16[192,384]{1,0:T(8,128)(2,1)S(1)} %get-tuple-element.107), channel_id=1, source_target_pairs={{0,3},{1,0},{2,1},{3,2},{4,7},{5,4},{6,5},{7,6},{8,11},{9,8},{10,9... | collective-permute-start | bytes 442376 | tf_op jit(solution)/shard_map/ppermute | solution.py:31
  390.9 17.9 %collective-permute-done.59 = bf16[384,384]{1,0:T(8,128)(2,1)S(1)} collective-permute-done((bf16[384,384]{1,0:T(8,128)(2,1)S(1)}, bf16[384,384]{1,0:T(8,128)(2,1)S(1)}, u32[]{:S(2)}, u32[]{:S(2)}) %collective-permute-start.59) | collective-permute-done | bytes 294944 | tf_op jit(solution)/shard_map/ppermute | solution.py:31
  416.8 4.8 %collective-permute-done.62.refs_2_ = bf16[384,384]{1,0:T(8,128)(2,1)S(1)} collective-permute-done((bf16[384,384]{1,0:T(8,128)(2,1)S(1)}, bf16[384,384]{1,0:T(8,128)(2,1)S(1)}, u32[]{:S(2)}, u32[]{:S(2)}) %collective-permute-start.62) | collective-permute-done | bytes 294944 | tf_op jit(solution)/shard_map/ppermute | solution.py:26
  456.1 4.5 reshape.189
  (299 shorter events, 155.1 us)
Async XLA Ops:
  7.3 39.6 %collective-permute-start.17 = (bf16[384,384]{1,0:T(8,128)(2,1)S(1)}, bf16[384,384]{1,0:T(8,128)(2,1)S(1)}, u32[]{:S(2)}, u32[]{:S(2)}) collective-permute-start(bf16[384,384]{1,0:T(8,128)(2,1)S(1)} %pad_maximum_fusion.5), channel_id=1, source_target_pairs={{0,1},{1,2},{2,3},{3,0},{4,5},{5,6},{6,7},{7,4},{8,9},{9,10},{10,1... | collective-permute-start | bytes 884744 | tf_op jit(solution)/shard_map/ppermute | solution.py:31
  8.6 38.3 %collective-permute-start.18 = (bf16[384,384]{1,0:T(8,128)(2,1)S(1)}, bf16[384,384]{1,0:T(8,128)(2,1)S(1)}, u32[]{:S(2)}, u32[]{:S(2)}) collective-permute-start(bf16[384,384]{1,0:T(8,128)(2,1)S(1)} %pad_maximum_fusion.5), channel_id=1, source_target_pairs={{0,2},{1,3},{2,0},{3,1},{4,6},{5,7},{6,4},{7,5},{8,10},{9,11},{10,... | collective-permute-start | bytes 884744 | tf_op jit(solution)/shard_map/ppermute | solution.py:31
  9.6 37.4 %collective-permute-start.19 = (bf16[384,384]{1,0:T(8,128)(2,1)S(1)}, bf16[384,384]{1,0:T(8,128)(2,1)S(1)}, u32[]{:S(2)}, u32[]{:S(2)}) collective-permute-start(bf16[384,384]{1,0:T(8,128)(2,1)S(1)} %pad_maximum_fusion.5), channel_id=1, source_target_pairs={{0,3},{1,0},{2,1},{3,2},{4,7},{5,4},{6,5},{7,6},{8,11},{9,8},{10,9... | collective-permute-start | bytes 884744 | tf_op jit(solution)/shard_map/ppermute | solution.py:31
  9.9 32.5 %collective-permute-start.4 = (bf16[192,384]{1,0:T(8,128)(2,1)S(1)}, bf16[192,384]{1,0:T(8,128)(2,1)}, u32[]{:S(2)}, u32[]{:S(2)}) collective-permute-start(bf16[192,384]{1,0:T(8,128)(2,1)S(1)} %get-tuple-element.86), channel_id=1, source_target_pairs={{0,2},{1,3},{2,0},{3,1},{4,6},{5,7},{6,4},{7,5},{8,10},{9,11},{10,... | collective-permute-start | bytes 442376 | tf_op jit(solution)/shard_map/ppermute | solution.py:31
  11.3 34.2 %collective-permute-start.5 = (bf16[192,384]{1,0:T(8,128)(2,1)S(1)}, bf16[192,384]{1,0:T(8,128)(2,1)S(1)}, u32[]{:S(2)}, u32[]{:S(2)}) collective-permute-start(bf16[192,384]{1,0:T(8,128)(2,1)S(1)} %get-tuple-element.86), channel_id=1, source_target_pairs={{0,3},{1,0},{2,1},{3,2},{4,7},{5,4},{6,5},{7,6},{8,11},{9,8},{10,9... | collective-permute-start | bytes 442376 | tf_op jit(solution)/shard_map/ppermute | solution.py:31
  47.1 54.3 %collective-permute-start.21 = (bf16[1536,384]{1,0:T(8,128)(2,1)S(1)}, bf16[1536,384]{1,0:T(8,128)(2,1)S(1)}, u32[]{:S(2)}, u32[]{:S(2)}) collective-permute-start(bf16[1536,384]{1,0:T(8,128)(2,1)S(1)} %bitcast.152), channel_id=1, source_target_pairs={{0,8},{4,12},{8,0},{12,4},{16,24},{20,28},{24,16},{28,20},{1,9},{5... | collective-permute-start | bytes 3538952 | tf_op jit(solution)/shard_map/ppermute | solution.py:26
  47.4 55.4 %collective-permute-start.23 = (bf16[1536,384]{1,0:T(8,128)(2,1)S(1)}, bf16[1536,384]{1,0:T(8,128)(2,1)}, u32[]{:S(2)}, u32[]{:S(2)}) collective-permute-start(bf16[1536,384]{1,0:T(8,128)(2,1)S(1)} %bitcast.153), channel_id=1, source_target_pairs={{0,16},{4,20},{8,24},{12,28},{16,0},{20,4},{24,8},{28,12},{1,17},{... | collective-permute-start | bytes 3538952 | tf_op jit(solution)/shard_map/ppermute | solution.py:26
  48.6 37.9 %collective-permute-start.9 = (bf16[768,384]{1,0:T(8,128)(2,1)S(1)}, bf16[768,384]{1,0:T(8,128)(2,1)}, u32[]{:S(2)}, u32[]{:S(2)}) collective-permute-start(bf16[768,384]{1,0:T(8,128)(2,1)S(1)} %bitcast.148), channel_id=1, source_target_pairs={{0,16},{4,20},{8,24},{12,28},{16,0},{20,4},{24,8},{28,12},{1,17},{... | collective-permute-start | bytes 1769480 | tf_op jit(solution)/shard_map/ppermute | solution.py:26
  60.2 30.9 %collective-permute-start.1 = (bf16[132,192]{1,0:T(8,128)(2,1)}, bf16[132,192]{1,0:T(8,128)(2,1)S(1)}, u32[]{:S(2)}, u32[]{:S(2)}) collective-permute-start(bf16[132,192]{1,0:T(8,128)(2,1)} %reshape.164), channel_id=1, source_target_pairs={{0,2},{1,3},{2,0},{3,1},{4,6},{5,7},{6,4},{7,5},{8,10},{9,11},{10,... | collective-permute-start | bytes 152072 | tf_op jit(solution)/shard_map/ppermute | solution.py:31
  61.2 31.6 %collective-permute-start.11 = (bf16[384,384]{1,0:T(8,128)(2,1)S(1)}, bf16[384,384]{1,0:T(8,128)(2,1)S(1)}, u32[]{:S(2)}, u32[]{:S(2)}) collective-permute-start(bf16[384,384]{1,0:T(8,128)(2,1)S(1)} %slice.198), channel_id=1, source_target_pairs={{0,16},{4,20},{8,24},{12,28},{16,0},{20,4},{24,8},{28,12},{1,17},{... | collective-permute-start | bytes 884744 | tf_op jit(solution)/shard_map/ppermute | solution.py:26
  102.8 32.4 %collective-permute-start.25 = (bf16[768,384]{1,0:T(8,128)(2,1)}, bf16[768,384]{1,0:T(8,128)(2,1)}, u32[]{:S(2)}, u32[]{:S(2)}) collective-permute-start(bf16[768,384]{1,0:T(8,128)(2,1)} %slice.200), channel_id=1, source_target_pairs={{0,16},{4,20},{8,24},{12,28},{16,0},{20,4},{24,8},{28,12},{1,17},{... | collective-permute-start | bytes 1769480 | tf_op jit(solution)/shard_map/ppermute | solution.py:26
  117.4 67.7 %collective-permute-start.20 = (bf16[1536,384]{1,0:T(8,128)(2,1)S(1)}, bf16[1536,384]{1,0:T(8,128)(2,1)}, u32[]{:S(2)}, u32[]{:S(2)}) collective-permute-start(bf16[1536,384]{1,0:T(8,128)(2,1)S(1)} %bitcast.154), channel_id=1, source_target_pairs={{0,4},{4,0},{8,12},{12,8},{16,20},{20,16},{24,28},{28,24},{1,5},{5... | collective-permute-start | bytes 3538952 | tf_op jit(solution)/shard_map/ppermute | solution.py:26
  118.0 67.1 %collective-permute-start.22 = (bf16[1536,384]{1,0:T(8,128)(2,1)}, bf16[1536,384]{1,0:T(8,128)(2,1)}, u32[]{:S(2)}, u32[]{:S(2)}) collective-permute-start(bf16[1536,384]{1,0:T(8,128)(2,1)} %copy-done.3), channel_id=1, source_target_pairs={{0,4},{4,0},{8,12},{12,8},{16,20},{20,16},{24,28},{28,24},{1,5},{5... | collective-permute-start | bytes 3538952 | tf_op jit(solution)/shard_map/ppermute | solution.py:26
  118.1 67.0 %collective-permute-start.24 = (bf16[1536,384]{1,0:T(8,128)(2,1)}, bf16[1536,384]{1,0:T(8,128)(2,1)}, u32[]{:S(2)}, u32[]{:S(2)}) collective-permute-start(bf16[1536,384]{1,0:T(8,128)(2,1)} %collective-permute-done.23.refs_2_), channel_id=1, source_target_pairs={{0,4},{4,0},{8,12},{12,8},{16,20},{20,16},{24,28},{28,24},{1,5},{5... | collective-permute-start | bytes 3538952 | tf_op jit(solution)/shard_map/ppermute | solution.py:26
  139.5 45.6 %collective-permute-start.27 = (bf16[1536,384]{1,0:T(8,128)(2,1)S(1)}, bf16[1536,384]{1,0:T(8,128)(2,1)}, u32[]{:S(2)}, u32[]{:S(2)}) collective-permute-start(bf16[1536,384]{1,0:T(8,128)(2,1)S(1)} %constant_dynamic-update-slice_fusion.2.refs_3_), channel_id=1, source_target_pairs={{0,4},{4,0},{8,12},{12,8},{16,20},{20,16},{24,28},{28,24},{1,5},{5... | collective-permute-start | bytes 3538952 | tf_op jit(solution)/shard_map/ppermute | solution.py:26
  202.5 109.4 %collective-permute-start.53 = (bf16[4,1536,384]{2,1,0:T(8,128)(2,1)}, bf16[4,1536,384]{2,1,0:T(8,128)(2,1)}, u32[]{:S(2)}, u32[]{:S(2)}) collective-permute-start(bf16[4,1536,384]{2,1,0:T(8,128)(2,1)} %get-tuple-element.82), channel_id=1, source_target_pairs={{0,4},{4,0},{8,12},{12,8},{16,20},{20,16},{24,28},{28,24},{1,5},{5... | collective-permute-start | bytes 14155784 | tf_op jit(solution)/shard_map/ppermute | solution.py:26
  229.1 36.8 %collective-permute-start.28 = (bf16[2,896,128]{2,1,0:T(8,128)(2,1)}, bf16[2,896,128]{2,1,0:T(8,128)(2,1)S(1)}, u32[]{:S(2)}, u32[]{:S(2)}) collective-permute-start(bf16[2,896,128]{2,1,0:T(8,128)(2,1)} %get-tuple-element.70), channel_id=1, source_target_pairs={{1,0},{2,1},{3,2},{5,4},{6,5},{7,6},{9,8},{10,9},{11,10},{13,12},{... | collective-permute-start | bytes 1376264 | tf_op jit(solution)/shard_map/ppermute | solution.py:37
  336.4 34.3 %collective-permute-start.55 = (bf16[1536,384]{1,0:T(8,128)(2,1)}, bf16[1536,384]{1,0:T(8,128)(2,1)}, u32[]{:S(2)}, u32[]{:S(2)}) collective-permute-start(bf16[1536,384]{1,0:T(8,128)(2,1)} %pad_maximum_fusion), channel_id=1, source_target_pairs={{0,8},{4,12},{8,0},{12,4},{16,24},{20,28},{24,16},{28,20},{1,9},{5... | collective-permute-start | bytes 3538952 | tf_op jit(solution)/shard_map/ppermute | solution.py:26
  337.8 43.8 %collective-permute-start.57 = (bf16[1536,384]{1,0:T(8,128)(2,1)}, bf16[1536,384]{1,0:T(8,128)(2,1)}, u32[]{:S(2)}, u32[]{:S(2)}) collective-permute-start(bf16[1536,384]{1,0:T(8,128)(2,1)} %pad_maximum_fusion.1), channel_id=1, source_target_pairs={{0,16},{4,20},{8,24},{12,28},{16,0},{20,4},{24,8},{28,12},{1,17},{... | collective-permute-start | bytes 3538952 | tf_op jit(solution)/shard_map/ppermute | solution.py:26
  343.2 41.4 %collective-permute-start.32 = (bf16[528,192]{1,0:T(8,128)(2,1)S(1)}, bf16[528,192]{1,0:T(8,128)(2,1)S(1)}, u32[]{:S(2)}, u32[]{:S(2)}) collective-permute-start(bf16[528,192]{1,0:T(8,128)(2,1)S(1)} %fusion.13), channel_id=1, source_target_pairs={{0,8},{4,12},{8,0},{12,4},{16,24},{20,28},{24,16},{28,20},{1,9},{5... | collective-permute-start | bytes 608264 | tf_op jit(solution)/shard_map/ppermute | solution.py:26
  347.3 39.5 %collective-permute-start.42 = (bf16[192,384]{1,0:T(8,128)(2,1)S(1)}, bf16[192,384]{1,0:T(8,128)(2,1)S(1)}, u32[]{:S(2)}, u32[]{:S(2)}) collective-permute-start(bf16[192,384]{1,0:T(8,128)(2,1)S(1)} %get-tuple-element.106), channel_id=1, source_target_pairs={{0,1},{1,2},{2,3},{3,0},{4,5},{5,6},{6,7},{7,4},{8,9},{9,10},{10,1... | collective-permute-start | bytes 442376 | tf_op jit(solution)/shard_map/ppermute | solution.py:31
  347.4 40.0 %collective-permute-start.43 = (bf16[192,384]{1,0:T(8,128)(2,1)S(1)}, bf16[192,384]{1,0:T(8,128)(2,1)S(1)}, u32[]{:S(2)}, u32[]{:S(2)}) collective-permute-start(bf16[192,384]{1,0:T(8,128)(2,1)S(1)} %get-tuple-element.108), channel_id=1, source_target_pairs={{0,2},{1,3},{2,0},{3,1},{4,6},{5,7},{6,4},{7,5},{8,10},{9,11},{10,... | collective-permute-start | bytes 442376 | tf_op jit(solution)/shard_map/ppermute | solution.py:31
  386.9 26.5 %collective-permute-start.60 = (bf16[384,384]{1,0:T(8,128)(2,1)S(1)}, bf16[384,384]{1,0:T(8,128)(2,1)S(1)}, u32[]{:S(2)}, u32[]{:S(2)}) collective-permute-start(bf16[384,384]{1,0:T(8,128)(2,1)S(1)} %get-tuple-element.100), channel_id=1, source_target_pairs={{0,3},{1,0},{2,1},{3,2},{4,7},{5,4},{6,5},{7,6},{8,11},{9,8},{10,9... | collective-permute-start | bytes 884744 | tf_op jit(solution)/shard_map/ppermute | solution.py:31
  388.8 26.6 %collective-permute-start.46 = (bf16[192,384]{1,0:T(8,128)(2,1)S(1)}, bf16[192,384]{1,0:T(8,128)(2,1)S(1)}, u32[]{:S(2)}, u32[]{:S(2)}) collective-permute-start(bf16[192,384]{1,0:T(8,128)(2,1)S(1)} %fusion.23.refs_0_), channel_id=1, source_target_pairs={{0,8},{4,12},{8,0},{12,4},{16,24},{20,28},{24,16},{28,20},{1,9},{5... | collective-permute-start | bytes 442376 | tf_op jit(solution)/shard_map/ppermute | solution.py:26
  (87 other events, 1148.6 us)
